TPU v7x, 32 devices: a whole 2x2x4 slice. The times are simulated.
32 devices in a mesh: dp: 8 (over z, x), sp: 4 (over y, core).
Axes of the slice: x: 2, y: 2, z: 4, core: 2. Of those that a mesh axis runs over, the one named last changes fastest.
Arguments:
- hidden_in: bfloat16 [8, 1024, 512], P('dp', 'sp'), may hold values from -6 to 6
- cotangent: float32 [8, 1024, 512], P('dp', 'sp'), may hold values from -6 to 6
- lengths: int32 [8], P('dp'), may hold values from 256 to 1024, as said below
- master: float32 [6301696], P(('dp', 'sp'))
- moment_one: float32 [6301696], P(('dp', 'sp'))
- moment_two: float32 [6301696], P(('dp', 'sp'))
Outputs:
- output: float32 [8, 1024, 512], P('dp', 'sp')
- input_grad: float32 [8, 1024, 512], P('dp', 'sp')
- new_master: float32 [6301696], P(('dp', 'sp'))
- new_moment_one: float32 [6301696], P(('dp', 'sp'))
- new_moment_two: float32 [6301696], P(('dp', 'sp'))
- new_weights: bfloat16 [6301696], P(('dp', 'sp'))
- grad_norm: float32 [], replicated
- gains_grad: float32 [2, 2, 512], replicated
Inputs may be any that keep to these rules, and one draw needn't show every extreme that they name: `lengths`: in every draw one sequence has all 1024 tokens real and another only 256.
All inputs are finite; a program needn't handle non-finite values.
Results may differ from a plain program's by a relative error of at most 0.017.
Values may be sent and summed in bfloat16 or wider, within the bound.
A program may use at most 192 MiB of HBM per device.

v0:
```python
import jax
import jax.numpy as jnp
from jax import lax
from jax.sharding import PartitionSpec as P

D = 512
HEADS = 8
HEAD_DIM = 64
FF = 1368
SEQ = 1024
BLOCK = 512
STEP = 5


NORM_EPS = 1e-06
ADAM_EPS = 1e-08
LEARN_RATE = 0.02
DECAY_RATE = 0.01


def shortened(array):

    def short(part):
        return part.astype(jnp.bfloat16) if part.dtype == jnp.float32 else part

    return jax.tree.map(short, array)


def layer_pieces(flat_weights, layer_index):
    shapes = [(D, 3 * D), (D, D), (D, 2 * FF), (FF, D), (2, D)]
    offset = layer_index * (4 * D * D + 3 * D * FF + 2 * D)
    pieces = []
    for dims_pair in shapes:
        length_now = dims_pair[0] * dims_pair[1]
        pieces.append(flat_weights[offset : offset + length_now].reshape(dims_pair))
        offset = offset + length_now
    return pieces


def rope_tables(positions):
    half_dim = HEAD_DIM // 2
    frequency = jnp.exp(
        -jnp.log(10000.0) * jnp.arange(half_dim).astype(jnp.float32) * 2.0 / HEAD_DIM
    )
    angles = positions.astype(jnp.float32)[:, None] * frequency[None, :]
    return (jnp.cos(angles), jnp.sin(angles))


def rotate(values, cosine_table, sine_table):
    half_dim = values.shape[-1] // 2
    first_half = values[..., :half_dim]
    second_half = values[..., half_dim:]
    cos_rows = cosine_table[:, None, :]
    sin_rows = sine_table[:, None, :]
    return jnp.concatenate(
        [
            first_half * cos_rows - second_half * sin_rows,
            second_half * cos_rows + first_half * sin_rows,
        ],
        axis=-1,
    )


def unrotate(values, cosine_table, sine_table):
    half_dim = values.shape[-1] // 2
    first_half = values[..., :half_dim]
    second_half = values[..., half_dim:]
    cos_rows = cosine_table[:, None, :]
    sin_rows = sine_table[:, None, :]
    return jnp.concatenate(
        [
            first_half * cos_rows + second_half * sin_rows,
            second_half * cos_rows - first_half * sin_rows,
        ],
        axis=-1,
    )


def norm_forward(stream, gain):
    factor = lax.rsqrt(jnp.mean(stream * stream, axis=-1, keepdims=True) + NORM_EPS)
    return (stream * factor * gain, factor)


def norm_backward(upstream, stream, factor, gain):
    scaled = upstream * gain
    gain_grad = jnp.sum(upstream * stream * factor, axis=(0, 1))
    stream_grad = factor * scaled - stream * factor**3 * jnp.mean(
        scaled * stream, axis=-1, keepdims=True
    )
    return (stream_grad, gain_grad)


def block_logits(query_block, key_rows, offset, length_now):
    raw_scores = jnp.einsum(
        "qhd,khd->hqk", query_block, key_rows, preferred_element_type=jnp.float32
    )
    row_place = offset + jnp.arange(query_block.shape[0])[:, None]
    col_place = jnp.arange(key_rows.shape[0])[None, :]
    allowed = (col_place <= row_place) & (col_place < length_now)
    return jnp.where(allowed[None], raw_scores * HEAD_DIM ** (-0.5), -1000000000.0)


def attend_forward(packed_in):
    sequence, length_now = packed_in
    query_rows = sequence[:, 0]
    key_rows = sequence[:, 1]
    value_rows = sequence[:, 2]
    context_parts = []
    logsum_parts = []
    for offset in range(0, SEQ, BLOCK):
        logits = block_logits(query_rows[offset : offset + BLOCK], key_rows, offset, length_now)
        logsum = jax.nn.logsumexp(logits, axis=-1)
        weights_soft = jnp.exp(logits - logsum[..., None]).astype(jnp.bfloat16)
        context_parts.append(
            jnp.einsum("hqk,khd->qhd", weights_soft, value_rows, preferred_element_type=jnp.float32)
        )
        logsum_parts.append(logsum)
    return (jnp.concatenate(context_parts, 0), jnp.concatenate(logsum_parts, 1))


def attend_backward(packed_in):
    sequence, grad_context, logsum, length_now = packed_in
    query_rows = sequence[:, 0]
    key_rows = sequence[:, 1]
    value_rows = sequence[:, 2]
    grad_rows = grad_context.reshape(query_rows.shape)
    key_grad = jnp.zeros(key_rows.shape, jnp.float32)
    value_grad = jnp.zeros(value_rows.shape, jnp.float32)
    query_parts = []
    for offset in range(0, SEQ, BLOCK):
        query_block = query_rows[offset : offset + BLOCK]
        grad_block = grad_rows[offset : offset + BLOCK]
        logits = block_logits(query_block, key_rows, offset, length_now)
        weights_soft = jnp.exp(logits - logsum[:, offset : offset + BLOCK, None])
        value_grad = value_grad + jnp.einsum(
            "hqk,qhd->khd",
            weights_soft.astype(jnp.bfloat16),
            grad_block,
            preferred_element_type=jnp.float32,
        )
        weight_grad = jnp.einsum(
            "qhd,khd->hqk", grad_block, value_rows, preferred_element_type=jnp.float32
        )
        centered = weight_grad - jnp.sum(weights_soft * weight_grad, axis=-1, keepdims=True)
        score_grad = (weights_soft * centered * HEAD_DIM ** (-0.5)).astype(jnp.bfloat16)
        query_parts.append(
            jnp.einsum("hqk,khd->qhd", score_grad, key_rows, preferred_element_type=jnp.float32)
        )
        key_grad = key_grad + jnp.einsum(
            "hqk,qhd->khd", score_grad, query_block, preferred_element_type=jnp.float32
        )
    query_grad = jnp.concatenate(query_parts, 0)
    return jnp.stack([query_grad, key_grad, value_grad], axis=1).astype(jnp.bfloat16)


def attention_forward(stream, weight_qkv, weight_out, cosine_table, sine_table, lengths):
    seq_count, row_count, feature_count = stream.shape
    groups = lax.axis_size("sp")
    head_local = HEADS // groups
    inputs_low = stream.astype(jnp.bfloat16).reshape(-1, feature_count)
    projected = jnp.dot(inputs_low, weight_qkv, preferred_element_type=jnp.float32).reshape(
        seq_count, row_count, 3, HEADS, HEAD_DIM
    )
    rotated = jnp.stack(
        [
            rotate(projected[:, :, 0], cosine_table, sine_table),
            rotate(projected[:, :, 1], cosine_table, sine_table),
            projected[:, :, 2],
        ],
        axis=2,
    )
    outgoing = rotated.astype(jnp.bfloat16).reshape(
        seq_count, row_count, 3, groups, head_local * HEAD_DIM
    )
    by_heads = lax.all_to_all(outgoing, "sp", split_axis=3, concat_axis=1, tiled=True)
    by_heads = by_heads.reshape(seq_count, row_count * groups, 3, head_local, HEAD_DIM)
    context, logsum = lax.map(attend_forward, (by_heads, lengths))
    context_low = context.astype(jnp.bfloat16).reshape(
        seq_count, row_count * groups, 1, head_local * HEAD_DIM
    )
    by_tokens = lax.all_to_all(context_low, "sp", split_axis=1, concat_axis=2, tiled=True)
    context_rows = by_tokens.reshape(-1, feature_count)
    branch = jnp.dot(context_rows, weight_out, preferred_element_type=jnp.float32).reshape(
        seq_count, row_count, feature_count
    )
    return (branch, (inputs_low, context_rows, by_heads, logsum))


def attention_backward(upstream, saved, weight_qkv, weight_out, cosine_table, sine_table, lengths):
    inputs_low, context_rows, by_heads, logsum = saved
    seq_count, row_count, feature_count = upstream.shape
    groups = lax.axis_size("sp")
    head_local = HEADS // groups
    upstream_low = upstream.astype(jnp.bfloat16).reshape(-1, feature_count)
    out_grad = jnp.einsum(
        "nd,ne->de", context_rows, upstream_low, preferred_element_type=jnp.float32
    )
    context_grad = jnp.dot(upstream_low, weight_out.T, preferred_element_type=jnp.float32).astype(
        jnp.bfloat16
    )
    context_grad = context_grad.reshape(seq_count, row_count, groups, head_local * HEAD_DIM)
    grad_heads = lax.all_to_all(context_grad, "sp", split_axis=2, concat_axis=1, tiled=True)
    head_grads = lax.map(attend_backward, (by_heads, grad_heads, logsum, lengths))
    outgoing = head_grads.reshape(seq_count, row_count * groups, 3, 1, head_local * HEAD_DIM)
    token_grads = lax.all_to_all(
        shortened(outgoing), "sp", split_axis=1, concat_axis=3, tiled=True
    ).astype(outgoing.dtype)
    token_grads = token_grads.reshape(seq_count, row_count, 3, HEADS, HEAD_DIM).astype(jnp.float32)
    lin_grad = jnp.stack(
        [
            unrotate(token_grads[:, :, 0], cosine_table, sine_table),
            unrotate(token_grads[:, :, 1], cosine_table, sine_table),
            token_grads[:, :, 2],
        ],
        axis=2,
    )
    lin_grad = lin_grad.astype(jnp.bfloat16).reshape(-1, 3 * feature_count)
    qkv_grad = jnp.einsum("nd,ne->de", inputs_low, lin_grad, preferred_element_type=jnp.float32)
    input_grad = jnp.dot(lin_grad, weight_qkv.T, preferred_element_type=jnp.float32).reshape(
        seq_count, row_count, feature_count
    )
    return (input_grad, qkv_grad, out_grad)


def ffn_forward(stream, weight_gu, weight_down):
    seq_count, row_count, feature_count = stream.shape
    inputs_low = stream.astype(jnp.bfloat16).reshape(-1, feature_count)
    both_parts = jnp.dot(inputs_low, weight_gu, preferred_element_type=jnp.float32)
    units = (jax.nn.silu(both_parts[:, :FF]) * both_parts[:, FF:]).astype(jnp.bfloat16)
    branch = jnp.dot(units, weight_down, preferred_element_type=jnp.float32).reshape(
        seq_count, row_count, feature_count
    )
    return (branch, (inputs_low, both_parts, units))


def ffn_backward(upstream, saved, weight_gu, weight_down):
    inputs_low, both_parts, units = saved
    seq_count, row_count, feature_count = upstream.shape
    upstream_low = upstream.astype(jnp.bfloat16).reshape(-1, feature_count)
    down_grad = jnp.einsum("nf,nd->fd", units, upstream_low, preferred_element_type=jnp.float32)
    units_grad = jnp.dot(upstream_low, weight_down.T, preferred_element_type=jnp.float32)
    gate_part = both_parts[:, :FF]
    up_part = both_parts[:, FF:]
    sigmoid_part = jax.nn.sigmoid(gate_part)
    gate_grad = units_grad * up_part * sigmoid_part * (1.0 + gate_part * (1.0 - sigmoid_part))
    up_grad = units_grad * gate_part * sigmoid_part
    both_grad = jnp.concatenate([gate_grad, up_grad], axis=1).astype(jnp.bfloat16)
    gu_grad = jnp.einsum("nd,nf->df", inputs_low, both_grad, preferred_element_type=jnp.float32)
    input_grad = jnp.dot(both_grad, weight_gu.T, preferred_element_type=jnp.float32).reshape(
        seq_count, row_count, feature_count
    )
    return (input_grad, gu_grad, down_grad)


def shards(hidden_in, cotangent, lengths, master, moment_one, moment_two):
    shard_low = master.astype(jnp.bfloat16)
    flat_weights = lax.all_gather(shard_low, ("dp", "sp"), axis=0, tiled=True)
    seq_count, row_count, feature_count = hidden_in.shape
    positions = lax.axis_index("sp") * row_count + jnp.arange(row_count)
    cosine_table, sine_table = rope_tables(positions)
    first_weights = layer_pieces(flat_weights, 0)
    second_weights = layer_pieces(flat_weights, 1)
    gains_first = first_weights[4].astype(jnp.float32)
    gains_second = second_weights[4].astype(jnp.float32)
    stream_zero = hidden_in.astype(jnp.float32)
    attn_zero, attn_zero_saved = attention_forward(
        stream_zero, first_weights[0], first_weights[1], cosine_table, sine_table, lengths
    )
    resid_one = stream_zero + attn_zero
    stream_one, factor_one = norm_forward(resid_one, gains_first[0])
    ffn_zero, ffn_zero_saved = ffn_forward(stream_one, first_weights[2], first_weights[3])
    resid_two = stream_one + ffn_zero
    stream_two, factor_two = norm_forward(resid_two, gains_first[1])
    normed_three, factor_three = norm_forward(stream_two, gains_second[0])
    attn_one, attn_one_saved = attention_forward(
        normed_three, second_weights[0], second_weights[1], cosine_table, sine_table, lengths
    )
    stream_three = stream_two + attn_one
    normed_four, factor_four = norm_forward(stream_three, gains_second[1])
    ffn_one, ffn_one_saved = ffn_forward(normed_four, second_weights[2], second_weights[3])
    output = stream_three + ffn_one
    keep = (positions[None, :] < lengths[:, None]).astype(jnp.float32)
    upstream = cotangent * keep[:, :, None]
    ffn_in_grad, gu_grad_one, down_grad_one = ffn_backward(
        upstream, ffn_one_saved, second_weights[2], second_weights[3]
    )
    norm_part, gain_grad_four = norm_backward(
        ffn_in_grad, stream_three, factor_four, gains_second[1]
    )
    three_grad = upstream + norm_part
    attn_in_grad, qkv_grad_one, out_grad_one = attention_backward(
        three_grad,
        attn_one_saved,
        second_weights[0],
        second_weights[1],
        cosine_table,
        sine_table,
        lengths,
    )
    norm_part, gain_grad_three = norm_backward(
        attn_in_grad, stream_two, factor_three, gains_second[0]
    )
    two_grad = three_grad + norm_part
    resid_two_grad, gain_grad_two = norm_backward(two_grad, resid_two, factor_two, gains_first[1])
    ffn_in_grad, gu_grad_zero, down_grad_zero = ffn_backward(
        resid_two_grad, ffn_zero_saved, first_weights[2], first_weights[3]
    )
    one_grad = resid_two_grad + ffn_in_grad
    resid_one_grad, gain_grad_one = norm_backward(one_grad, resid_one, factor_one, gains_first[0])
    attn_in_grad, qkv_grad_zero, out_grad_zero = attention_backward(
        resid_one_grad,
        attn_zero_saved,
        first_weights[0],
        first_weights[1],
        cosine_table,
        sine_table,
        lengths,
    )
    input_grad = resid_one_grad + attn_in_grad
    gains_first_grad = jnp.stack([gain_grad_one, gain_grad_two])
    gains_second_grad = jnp.stack([gain_grad_three, gain_grad_four])
    grad_flat = jnp.concatenate(
        [
            qkv_grad_zero.reshape(-1),
            out_grad_zero.reshape(-1),
            gu_grad_zero.reshape(-1),
            down_grad_zero.reshape(-1),
            gains_first_grad.reshape(-1),
            qkv_grad_one.reshape(-1),
            out_grad_one.reshape(-1),
            gu_grad_one.reshape(-1),
            down_grad_one.reshape(-1),
            gains_second_grad.reshape(-1),
        ]
    )
    grad_grid = grad_flat.reshape(lax.axis_size("dp"), lax.axis_size("sp"), -1)
    partial_sum = lax.psum_scatter(
        grad_grid.astype(jnp.bfloat16), "sp", scatter_dimension=1, tiled=True
    ).astype(jnp.float32)
    grad_shard = lax.psum_scatter(partial_sum, "dp", scatter_dimension=0, tiled=True).reshape(-1)
    gains_local = jnp.stack([gains_first_grad, gains_second_grad])
    squares, gains_grad = lax.psum((jnp.sum(grad_shard * grad_shard), gains_local), ("dp", "sp"))
    grad_norm = jnp.sqrt(squares)
    clipped = grad_shard * jnp.minimum(1.0, 1.0 / grad_norm)
    new_one = 0.5 * moment_one + 0.5 * clipped
    new_two = 0.5 * moment_two + 0.5 * clipped * clipped
    correction = 1.0 - 0.5**STEP
    new_master = master * (1.0 - LEARN_RATE * DECAY_RATE) - LEARN_RATE * (new_one / correction) / (
        jnp.sqrt(new_two / correction) + ADAM_EPS
    )
    return (
        output,
        input_grad,
        new_master,
        new_one,
        new_two,
        new_master.astype(jnp.bfloat16),
        grad_norm,
        gains_grad,
    )


def solution(mesh):
    in_specs = (
        P("dp", "sp", None),
        P("dp", "sp", None),
        P("dp"),
        P(("dp", "sp")),
        P(("dp", "sp")),
        P(("dp", "sp")),
    )
    out_specs = (
        P("dp", "sp", None),
        P("dp", "sp", None),
        P(("dp", "sp")),
        P(("dp", "sp")),
        P(("dp", "sp")),
        P(("dp", "sp")),
        P(),
        P(),
    )
    return jax.shard_map(shards, mesh=mesh, in_specs=in_specs, out_specs=out_specs, check_vma=False)
```

profile of v0, /device:TPU:0, one launch (start us, length us, event | category | flops | bytes accessed | tf_op | source)
XLA Modules:
  0.0 1094.6 jit_solution(13723838610632103288)
XLA Ops:
  13.1 7.3 dynamic-update-slice
  22.6 232.7 %all-reduce.7.cloned.1.call-done = bf16[6301696]{0:T(1024)(128)(2,1)} async-done(((bf16[6301696]{0:T(1024)(128)(2,1)}), bf16[6301696]{0:T(1024)(128)(2,1)}) %all-reduce.7.cloned.1.call-update) | async-done | bytes 12603408
  295.4 13.9 %slice.340 = bf16[1368,512]{1,0:T(8,128)(2,1)} reshape(bf16[700416]{0:T(1024)(128)(2,1)} %get-tuple-element.90) | data formatting | bytes 2801664 | tf_op jit(solution)/shard_map/slice | solution.py:35
  327.5 6.0 all-to-all-done.1
  341.2 14.3 %all_to_all.108 = bf16[1,256,3,4,128]{1,4,2,0,3:T(8,128)(2,1)S(1)} all-to-all(bf16[1,256,3,4,128]{1,4,2,0,3:T(8,128)(2,1)S(1)} %pad_maximum_fusion.9), channel_id=1, replica_groups=mesh['dp'=8,'sp'=4] {'sp'}, dimensions={3} | all-to-all | bytes 1572864 | tf_op jit(solution)/shard_map/all_to_all | solution.py:175
  383.1 7.2 reshape.1055
  409.4 9.3 all_to_all.109
  430.9 12.8 %fusion.22 = f32[2,64,1024]{2,1,0:T(8,128)} fusion(f32[2,512,1024]{2,1,0:T(8,128)} %fusion.143, bf16[1024,3,2,64]{0,3,2,1:T(8,128)(2,1)} %squeeze.98, f32[2,512,1024]{2,1,0:T(8,128)} %get-tuple-element.167, f32[2,512]{1,0:T(2,128)S(1)} %log_add_fusion.1, pred[512,1024]{1,0:T(8,128)(4,1)S(1)} %copy-done.23), kind=kOutput, calls=%fused_computation.39 | convolution fusion | flops 145754112 | bytes 18489344 | tf_op jit(solution)/shard_map/while/body/eval_jaxpr/hqk,qhd->khd/dot_general | solution.py:149
  443.7 12.5 %fusion.91 = bf16[512,2,64]{0,2,1:T(8,128)(2,1)} fusion(f32[2,512,1024]{2,1,0:T(8,128)} %fusion.143, bf16[1024,3,2,64]{0,3,2,1:T(8,128)(2,1)} %squeeze.98, f32[2,512,1024]{2,1,0:T(8,128)} %get-tuple-element.167, f32[2,512]{1,0:T(2,128)S(1)} %log_add_fusion.1, pred[512,1024]{1,0:T(8,128)(4,1)S(1)} %copy-done.23), kind=kOutput, calls=%fused_computation.109 | convolution fusion | flops 145819648 | bytes 18227200 | tf_op jit(solution)/shard_map/while/body/eval_jaxpr/hqk,khd->qhd/dot_general | solution.py:147
  468.6 12.2 %fusion.94 = bf16[512,2,64]{0,2,1:T(8,128)(2,1)} fusion(f32[2,512,1024]{2,1,0:T(8,128)} %fusion.142, bf16[1024,3,2,64]{0,3,2,1:T(8,128)(2,1)} %squeeze.98, f32[2,512,1024]{2,1,0:T(8,128)} %copy-done.31, f32[2,512]{1,0:T(2,128)S(1)} %log_add_fusion, pred[512,1024]{1,0:T(8,128)(4,1)S(1)} %copy-done.22), kind=kOutput, calls=%fused_computation.110 | convolution fusion | flops 145819648 | bytes 18227200 | tf_op jit(solution)/shard_map/while/body/eval_jaxpr/hqk,khd->qhd/dot_general | solution.py:147
  480.9 12.6 %fusion.73 = bf16[2,64,1024]{2,1,0:T(8,128)(2,1)} fusion(f32[2,64,1024]{2,1,0:T(8,128)} %fusion.22, f32[2,512,1024]{2,1,0:T(8,128)} %fusion.142, bf16[1024,3,2,64]{0,3,2,1:T(8,128)(2,1)} %squeeze.98, f32[2,512,1024]{2,1,0:T(8,128)} %copy-done.31, f32[2,512]{1,0:T(2,128)S(1)} %log_add_fusion, pred[512,1024]{1,0:T(8,128)(4,1)S(1)} %copy-done.22), kind=kOutput, calls=%fused_computation.95 | convolution fusion | flops 146016256 | bytes 18751488 | tf_op jit(solution)/shard_map/while/body/eval_jaxpr/hqk,qhd->khd/dot_general | solution.py:149
  518.5 6.4 reshape.1072
  565.1 13.1 %fusion.34 = f32[2,64,1024]{2,1,0:T(8,128)} fusion(f32[2,512,1024]{2,1,0:T(8,128)} %fusion.139, bf16[1024,3,2,64]{0,3,2,1:T(8,128)(2,1)} %copy-done.41, f32[2,512,1024]{2,1,0:T(8,128)} %copy-done.30, f32[2,512]{1,0:T(2,128)S(1)} %log_add_fusion.3, pred[512,1024]{1,0:T(8,128)(4,1)} %get-tuple-element.154), kind=kOutput, calls=%fused_computation.43 | convolution fusion | flops 145754112 | bytes 18489344 | tf_op jit(solution)/shard_map/while/body/eval_jaxpr/hqk,qhd->khd/dot_general | solution.py:149
  578.2 12.8 %fusion.97 = bf16[512,2,64]{0,2,1:T(8,128)(2,1)} fusion(f32[2,512,1024]{2,1,0:T(8,128)} %fusion.139, bf16[1024,3,2,64]{0,3,2,1:T(8,128)(2,1)} %copy-done.41, f32[2,512,1024]{2,1,0:T(8,128)} %copy-done.30, f32[2,512]{1,0:T(2,128)S(1)} %log_add_fusion.3, pred[512,1024]{1,0:T(8,128)(4,1)} %get-tuple-element.154), kind=kOutput, calls=%fused_computation.111 | convolution fusion | flops 145819648 | bytes 18227200 | tf_op jit(solution)/shard_map/while/body/eval_jaxpr/hqk,khd->qhd/dot_general | solution.py:147
  597.1 12.3 %fusion.100 = bf16[512,2,64]{0,2,1:T(8,128)(2,1)} fusion(f32[2,512,1024]{2,1,0:T(8,128)} %fusion.138, bf16[1024,3,2,64]{0,3,2,1:T(8,128)(2,1)} %copy-done.41, f32[2,512,1024]{2,1,0:T(8,128)} %copy-done.28, f32[2,512]{1,0:T(2,128)S(1)} %log_add_fusion.2, pred[512,1024]{1,0:T(8,128)(4,1)S(1)} %copy-done.22), kind=kOutput, calls=%fused_computation.112 | convolution fusion | flops 145819648 | bytes 18227200 | tf_op jit(solution)/shard_map/while/body/eval_jaxpr/hqk,khd->qhd/dot_general | solution.py:147
  609.4 12.0 %fusion.76 = bf16[2,64,1024]{2,1,0:T(8,128)(2,1)S(1)} fusion(f32[2,64,1024]{2,1,0:T(8,128)} %fusion.34, f32[2,512,1024]{2,1,0:T(8,128)} %fusion.138, bf16[1024,3,2,64]{0,3,2,1:T(8,128)(2,1)} %copy-done.41, f32[2,512,1024]{2,1,0:T(8,128)} %copy-done.28, f32[2,512]{1,0:T(2,128)S(1)} %log_add_fusion.2, pred[512,1024]{1,0:T(8,128)(4,1)S(1)} %copy-done.22), kind=kOutput, calls=%fused_computation.96 | convolution fusion | flops 146016256 | bytes 18751488 | tf_op jit(solution)/shard_map/while/body/eval_jaxpr/hqk,qhd->khd/dot_general | solution.py:149
  638.3 6.5 reshape.1067
  673.9 23.6 %convert_element_type.303 = bf16[8,4,196928]{2,1,0:T(4,128)(2,1)} reshape(bf16[6301696]{0:T(1024)(128)(2,1)} %constant_dynamic-update-slice_fusion) | data formatting | bytes 25206784 | tf_op jit(solution)/shard_map/convert_element_type | solution.py:338
  697.5 11.5 %copy.135 = bf16[8,4,196928]{2,0,1:T(8,128)(2,1)} copy(bf16[8,4,196928]{2,1,0:T(4,128)(2,1)} %convert_element_type.303) | data formatting | bytes 25206784 | tf_op jit(solution)/shard_map/convert_element_type | solution.py:338
  709.0 99.6 %reduce-scatter.4.cloned.1.call-done = bf16[8,1,196928]{2,0,1:T(8,128)(2,1)} async-done(((bf16[8,4,196928]{2,0,1:T(8,128)(2,1)}), bf16[8,1,196928]{2,0,1:T(8,128)(2,1)}) %reduce-scatter.4.cloned.1.call-update) | async-done | bytes 3150864
  808.6 6.9 copy.136
  819.8 209.4 %all-reduce.9.cloned.1.call-done = f32[8,1,196928]{2,1,0:T(1,128)} async-done(((f32[8,1,196928]{2,1,0:T(1,128)}), f32[8,1,196928]{2,1,0:T(1,128)}) %all-reduce.9.cloned.1.call-update) | async-done | bytes 6301712
  1034.5 39.0 %all-reduce.3 = (f32[]{:T(128)}, f32[2,2,512]{2,1,0:T(2,128)}) all-reduce(f32[]{:T(128)} %multiply_reduce_fusion.5, f32[2,2,512]{2,1,0:T(2,128)S(1)} %pad_maximum_fusion.20), channel_id=1, replica_groups=mesh['dp'=8,'sp'=4] {'dp','sp'}, use_global_device_ids=true, to_apply=%region_27.28 | all-reduce | flops 2049 | bytes 16392 | tf_op jit(solution)/shard_map/psum | solution.py:342
  1074.2 9.0 multiply_reduce_fusion.4
  (317 shorter events, 274.0 us)
Async XLA Ops:
  7.2 248.2 %all-reduce.7.cloned.1.call-start = ((), (), s32[]{:S(2)}) async-start(), calls=%async_computation.9 | async-start | bytes 25206784
  22.6 343.5 %copy-start.21 = (pred[512,1024]{1,0:T(8,128)(4,1)}, pred[512,1024]{1,0:T(8,128)(4,1)S(1)}, u32[]{:S(2)}) copy-start(pred[512,1024]{1,0:T(8,128)(4,1)S(1)} %get-tuple-element.155) | copy-start | bytes 1572868
  267.5 42.5 %all-to-all-start = ((bf16[1,256,3,4,128]{1,4,2,0,3:T(8,128)(2,1)}), bf16[1,256,3,4,128]{1,4,2,0,3:T(8,128)(2,1)}, u32[]{:S(2)}, u32[]{:S(2)}) async-start(bf16[1,256,3,4,128]{1,4,2,0,3:T(8,128)(2,1)} %pad_maximum_fusion.8), calls=%async_computation | async-start | bytes 1572864 | tf_op jit(solution)/shard_map/all_to_all | solution.py:175
  295.4 38.6 %copy-start.26 = (bf16[512,512]{1,0:T(8,128)(2,1)}, bf16[512,512]{1,0:T(8,128)(2,1)S(1)}, u32[]{:S(2)}) copy-start(bf16[512,512]{1,0:T(8,128)(2,1)S(1)} %slice.333) | copy-start | bytes 1572868
  312.3 6.1 copy-start.41
  319.7 14.3 %copy-start.39 = (bf16[1,256,512]{2,1,0:T(8,128)(2,1)S(1)}, bf16[1,256,512]{2,1,0:T(8,128)(2,1)}, u32[]{:S(2)}) copy-start(bf16[1,256,512]{2,1,0:T(8,128)(2,1)} %param.6) | copy-start | bytes 786436
  324.1 9.4 all-to-all-start.1
  377.3 16.6 %all-to-all-start.3 = ((bf16[4,2,16384]{2,1,0:T(2,128)(2,1)}), bf16[4,2,16384]{2,1,0:T(2,128)(2,1)}, u32[]{:S(2)}, u32[]{:S(2)}) async-start(bf16[4,2,16384]{2,1,0:T(2,128)(2,1)} %reshape.1086), calls=%async_computation.3 | async-start | bytes 524288 | tf_op jit(solution)/shard_map/all_to_all | solution.py:181
  383.1 14.5 %copy-start.24 = (bf16[512,512]{1,0:T(8,128)(2,1)}, bf16[512,512]{1,0:T(8,128)(2,1)S(1)}, u32[]{:S(2)}) copy-start(bf16[512,512]{1,0:T(8,128)(2,1)S(1)} %slice.359) | copy-start | bytes 1572868
  456.1 7.2 copy-start.22
  503.2 25.4 %all-to-all-start.5 = ((bf16[1,1024,3,1,128]{4,2,3,0,1:T(4,128)(2,1)}), bf16[1,1024,3,1,128]{4,2,3,0,1:T(4,128)(2,1)}, u32[]{:S(2)}, u32[]{:S(2)}) async-start(bf16[1,1024,3,1,128]{4,2,3,0,1:T(4,128)(2,1)} %pad_maximum_fusion.2), calls=%async_computation.5 | async-start | bytes 2097152 | tf_op jit(solution)/shard_map/all_to_all | solution.py:205
  541.9 90.1 %copy-start.8 = (f32[1,256,512]{2,1,0:T(8,128)}, f32[1,256,512]{2,1,0:T(8,128)S(1)}, u32[]{:S(2)}) copy-start(f32[1,256,512]{2,1,0:T(8,128)S(1)} %multiply_subtract_fusion) | copy-start | bytes 1572868
  546.4 10.2 all-to-all-start.6
  621.4 10.6 copy-start.37
  627.7 22.7 %all-to-all-start.7 = ((bf16[1,1024,3,1,128]{4,2,3,0,1:T(4,128)(2,1)}), bf16[1,1024,3,1,128]{4,2,3,0,1:T(4,128)(2,1)}, u32[]{:S(2)}, u32[]{:S(2)}) async-start(bf16[1,1024,3,1,128]{4,2,3,0,1:T(4,128)(2,1)} %pad_maximum_fusion.3), calls=%async_computation.7 | async-start | bytes 2097152 | tf_op jit(solution)/shard_map/all_to_all | solution.py:205
  631.9 176.7 %reduce-scatter.4.cloned.1.call-start = ((), (), s32[]{:S(2)}) async-start(), calls=%async_computation.11 | async-start | bytes 15759360
  638.3 6.5 copy-start.16
  638.3 8.4 copy-start.35
  655.7 9.1 copy-start.7
  660.2 6.4 copy-start.20
  709.0 320.2 %all-reduce.9.cloned.1.call-start = ((), (), s32[]{:S(2)}) async-start(), calls=%async_computation.10 | async-start | bytes 12607488
  815.5 217.5 %copy-start.1 = (bf16[512,1536]{1,0:T(8,128)(2,1)S(1)}, bf16[512,1536]{1,0:T(8,128)(2,1)}, u32[]{:S(2)}) copy-start(bf16[512,1536]{1,0:T(8,128)(2,1)} %copy-done) | copy-start | bytes 4718596
  815.5 217.5 %copy-start.9 = (f32[1,256,512]{2,1,0:T(8,128)S(1)}, f32[1,256,512]{2,1,0:T(8,128)}, u32[]{:S(2)}) copy-start(f32[1,256,512]{2,1,0:T(8,128)} %copy-done.8) | copy-start | bytes 1572868
  815.5 217.5 %copy-start.11 = (bf16[1,256,3,8,64]{1,4,3,2,0:T(8,128)(2,1)S(1)}, bf16[1,256,3,8,64]{1,4,3,2,0:T(8,128)(2,1)}, u32[]{:S(2)}) copy-start(bf16[1,256,3,8,64]{1,4,3,2,0:T(8,128)(2,1)} %copy-done.10) | copy-start | bytes 2359300
  (39 other events, 109.1 us)
Sparse Core Ops, SparseCore 0:
  20.5 234.8 all-reduce.6
  709.1 99.4 reduce-scatter.3
  815.7 213.3 all-reduce.8
where the time goes:
time: 1100 us; the launch traced here: 1090 us
  waiting for transfers between devices  548 us (50%)
  local copies, waits for them, and re-layouts  212 us (19%)
  matrix products  180 us (16%)
  blocking collectives  62.5 us (6%)
  other arithmetic  48.7 us (4%)
  starting transfers between devices  25.3 us (2%)
  between operations  17.7 us (2%)
    unnamed x6, waiting for transfers between devices  542 us
    dot_general x4, matrix products, attend_backward(): jnp.einsum('hqk,qhd->khd', score_grad, query_block, preferred_element_typ...  50.6 us
    dot_general x4, matrix products, attend_backward(): jnp.einsum('hqk,khd->qhd', score_grad, key_rows, preferred_element_type=j...  49.8 us
    unnamed x133, local copies, waits for them, and re-layouts  40.6 us
    psum x1, blocking collectives, shards(): lax.psum((jnp.sum(grad_shard * grad_shard), gains_local), ('dp', 'sp'))  39 us
    convert_element_type x2, local copies, waits for them, and re-layouts, shards(): grad_grid.astype(jnp.bfloat16)  35.1 us
    slice x8, local copies, waits for them, and re-layouts, layer_pieces(): pieces.append(flat_weights[offset:offset + length_now].reshape(dims_pair))  33.6 us
  transfers between devices with their start and end apart: 9, of which 5 were waited for; matrix products, arithmetic and copies ran while one was open for 9% of the time, Pallas kernels for 0%

commit v1 on v0

v1 whole, which is shorter than its diff:
```python
import functools

import jax
import jax.numpy as jnp
from jax import lax
from jax.experimental import pallas as pl
from jax.experimental.pallas import tpu as pltpu
from jax.sharding import PartitionSpec as P

D = 512
HEADS = 8
HEAD_DIM = 64
FF = 1368
FFP = 1408
TILES = 11
STEP = 5
NORM_EPS = 1e-06
ADAM_EPS = 1e-08
LEARN_RATE = 0.02
DECAY_RATE = 0.01
LANES = 128
LAYER_ROWS = 24616
BASE_OUT = 6144
BASE_GU = 8192
BASE_DOWN = 19136
BASE_GAINS = 24608
GU_ROW = 2 * FF
PERIOD = 171
MESH = pl.DeviceIdType.MESH
MIB = 1 << 20
f32 = jnp.float32
bf16 = jnp.bfloat16


def mm(a, b):
    return lax.dot_general(a, b, (((1,), (0,)), ((), ())), preferred_element_type=f32)


def mm_nt(a, b):
    return lax.dot_general(a, b, (((1,), (1,)), ((), ())), preferred_element_type=f32)


def mm_tn(a, b):
    return lax.dot_general(a, b, (((0,), (0,)), ((), ())), preferred_element_type=f32)


def chunk_rows(rows):
    tiles = rows // 16
    best = max(d for d in range(1, 17) if tiles % d == 0)
    return best * 16


def vmem_spec():
    return pl.BlockSpec(memory_space=pltpu.VMEM)


def any_spec():
    return pl.BlockSpec(memory_space=pl.ANY)


def local_call(body, outs, ins, scratch=(), limit=60, flops=0):
    return pl.pallas_call(
        body,
        out_shape=[jax.ShapeDtypeStruct(s, d) for s, d in outs],
        in_specs=[vmem_spec()] * len(ins),
        out_specs=[vmem_spec()] * len(outs),
        scratch_shapes=list(scratch),
        compiler_params=pltpu.CompilerParams(vmem_limit_bytes=limit * MIB),
    )(*ins)


def coords():
    dp = lax.axis_index("dp")
    sp = lax.axis_index("sp")
    return lax.div(dp, 2), lax.rem(dp, 2), lax.div(sp, 2), lax.rem(sp, 2)


def place(z, x, y, c):
    return {"dp": z * 2 + x, "sp": y * 2 + c}


def remote(src, dst, send_sem, recv_sem, device):
    return pltpu.make_async_remote_copy(
        src_ref=src,
        dst_ref=dst,
        send_sem=send_sem,
        recv_sem=recv_sem,
        device_id=device,
        device_id_type=MESH,
    )


def order_at(tau, z):
    step = lax.div(tau + 1, 2)
    return z + jnp.where(lax.rem(tau, 2) == 1, -step, step)


def gather_weights(master_pad, zn, rows, share, zlo, zhi):
    nz = zhi - zlo
    half = rows // 2
    step = chunk_rows(rows)

    def body(x_ref, out_ref, own, send, recv, lsem):
        z, x, y, c = coords()
        bar = pltpu.get_barrier_semaphore()

        def hello(device):
            pl.semaphore_signal(bar, inc=1, device_id=device, device_id_type=MESH)

        hello(place(z, 1 - x, y, c))
        hello(place(z, x, 1 - y, c))
        hello(place(z, x, y, 1 - c))
        pl.when(z > 0)(lambda: hello(place(z - 1, x, y, c)))
        pl.when(z < zn - 1)(lambda: hello(place(z + 1, x, y, c)))

        shift = lax.rem(share * (((z * 2 + x) * 2 + y) * 2 + c), LANES)
        lane = lax.broadcasted_iota(jnp.int32, (step, LANES), 1)

        def align(i, carry):
            now = pltpu.roll(x_ref[pl.ds(8 + i * step, step), :], shift, 1)
            before = pltpu.roll(x_ref[pl.ds(7 + i * step, step), :], shift, 1)
            own[pl.ds(i * step, step), :] = jnp.where(lane >= shift, now, before).astype(bf16)
            return carry

        lax.fori_loop(0, rows // step, align, 0)
        pl.semaphore_wait(
            bar, 3 + (z > 0).astype(jnp.int32) + (z < zn - 1).astype(jnp.int32)
        )

        def slot(zp, xp, yp, cp):
            return (((zp - zlo) * 2 + xp) * 2 + yp) * 2 + cp

        def whole(zp, xp, yp):
            return out_ref.at[slot(zp, xp, yp, c)]

        def upper(zp, xp, yp):
            return out_ref.at[slot(zp, xp, yp, c), pl.ds(0, half)]

        def lower(zp, xp, yp):
            return out_ref.at[slot(zp, xp, yp, c), pl.ds(half, half)]

        to_x = place(z, 1 - x, y, c)
        to_y = place(z, x, 1 - y, c)
        to_c = place(z, x, y, 1 - c)

        def cp(ref, zp, s, r, device):
            return remote(ref, ref, send.at[zp - zlo, s], recv.at[zp - zlo, r], device)

        def right(zp):
            return cp(whole(zp, x, y), zp, 0, 0, place(z + 1, x, y, c))

        def left(zp):
            return cp(whole(zp, x, y), zp, 1, 0, place(z - 1, x, y, c))

        def first(zp):
            ref = whole(zp, x, y)
            return [cp(ref, zp, 2, 1, to_x), cp(ref, zp, 3, 2, to_y), cp(ref, zp, 4, 3, to_c)]

        def second_x(zp):
            return [
                cp(upper(zp, 1 - x, y), zp, 5, 4, to_y),
                cp(whole(zp, 1 - x, y), zp, 6, 6, to_c),
            ]

        def second_y(zp):
            return [
                cp(lower(zp, x, 1 - y), zp, 7, 5, to_x),
                cp(whole(zp, x, 1 - y), zp, 8, 7, to_c),
            ]

        def third_a(zp):
            return cp(upper(zp, 1 - x, 1 - y), zp, 9, 8, to_c)

        def third_b(zp):
            return cp(lower(zp, 1 - x, 1 - y), zp, 10, 9, to_c)

        def arrival(ref, zp, r):
            cp(ref, zp, 0, r, to_c).wait_recv()

        mine = (z >= zlo) & (z < zhi)

        @pl.when(mine)
        def _():
            keep = pltpu.make_async_copy(own, whole(z, x, y), lsem)
            keep.start()
            keep.wait()

        def valid(zp):
            return (zp >= zlo) & (zp < zhi)

        def stage_one(tau):
            zp = order_at(tau, z)

            @pl.when(valid(zp))
            def _():
                pl.when(tau > 0)(lambda: arrival(whole(zp, x, y), zp, 0))
                pl.when((zp <= z) & (z < zn - 1))(lambda: right(zp).start())
                pl.when((zp >= z) & (z > 0))(lambda: left(zp).start())
                for item in first(zp):
                    item.start()

        def stage_two(tau):
            zp = order_at(tau, z)

            @pl.when((tau >= 0) & valid(zp))
            def _():
                arrival(whole(zp, 1 - x, y), zp, 1)
                for item in second_x(zp):
                    item.start()
                arrival(whole(zp, x, 1 - y), zp, 2)
                for item in second_y(zp):
                    item.start()

        def stage_three(tau):
            zp = order_at(tau, z)

            @pl.when((tau >= 0) & valid(zp))
            def _():
                arrival(upper(zp, 1 - x, 1 - y), zp, 4)
                third_a(zp).start()
                arrival(lower(zp, 1 - x, 1 - y), zp, 5)
                third_b(zp).start()

        total = 2 * zn - 1

        def turn(tau, carry):
            pl.when(tau < total)(lambda: stage_one(tau))
            pl.when(tau - 1 < total)(lambda: stage_two(tau - 1))
            stage_three(tau - 2)
            return carry

        lax.fori_loop(0, total + 2, turn, 0)

        def finish(i, carry):
            zp = zlo + i
            pl.when((zp <= z) & (z < zn - 1))(lambda: right(zp).wait_send())
            pl.when((zp >= z) & (z > 0))(lambda: left(zp).wait_send())
            for item in first(zp) + second_x(zp) + second_y(zp) + [third_a(zp), third_b(zp)]:
                item.wait_send()
            far = 1 - c
            arrival(out_ref.at[slot(zp, x, y, far)], zp, 3)
            arrival(out_ref.at[slot(zp, 1 - x, y, far)], zp, 6)
            arrival(out_ref.at[slot(zp, x, 1 - y, far)], zp, 7)
            arrival(out_ref.at[slot(zp, 1 - x, 1 - y, far), pl.ds(0, half)], zp, 8)
            arrival(out_ref.at[slot(zp, 1 - x, 1 - y, far), pl.ds(half, half)], zp, 9)
            return carry

        lax.fori_loop(0, nz, finish, 0)

    return pl.pallas_call(
        body,
        out_shape=jax.ShapeDtypeStruct((nz * 8, rows, LANES), bf16),
        in_specs=[vmem_spec()],
        out_specs=any_spec(),
        scratch_shapes=[
            pltpu.VMEM((rows, LANES), bf16),
            pltpu.SemaphoreType.DMA((nz, 11)),
            pltpu.SemaphoreType.DMA((nz, 10)),
            pltpu.SemaphoreType.DMA,
        ],
        compiler_params=pltpu.CompilerParams(
            collective_id=1, has_side_effects=True, vmem_limit_bytes=40 * MIB
        ),
    )(master_pad)


def unpack_weights(slots, layer, rows, share):
    per_layer = slots.shape[0] // 2
    step = chunk_rows(rows)
    depth = LAYER_ROWS + rows

    def body(s_ref, qkv_ref, out_ref, gu_ref, down_ref, gains_ref, flat, gate_up):
        i = pl.program_id(0)
        start = lax.div(share * i, LANES)
        shift = lax.rem(share * i, LANES)
        edge = flat[pl.ds(start, 1), :]

        def fill(j, carry):
            flat[pl.ds(start + j * step, step), :] = s_ref[0, pl.ds(j * step, step), :].astype(f32)
            return carry

        lax.fori_loop(0, rows // step, fill, 0)

        @pl.when(shift > 0)
        def _():
            flat[pl.ds(start, 1), :] = flat[pl.ds(start, 1), :] + edge

        @pl.when(i == per_layer - 1)
        def _():
            for col in range(12):
                qkv_ref[:, 128 * col : 128 * col + 128] = flat[
                    pl.ds(col, D, stride=12), :
                ].astype(bf16)
            for col in range(4):
                out_ref[:, 128 * col : 128 * col + 128] = flat[
                    pl.ds(BASE_OUT + col, D, stride=4), :
                ].astype(bf16)
                down_ref[0:FF, 128 * col : 128 * col + 128] = flat[
                    pl.ds(BASE_DOWN + col, FF, stride=4), :
                ].astype(bf16)
                gains_ref[:, 128 * col : 128 * col + 128] = flat[
                    pl.ds(BASE_GAINS + col, 2, stride=4), :
                ]
            down_ref[FF:FFP, :] = jnp.zeros((FFP - FF, D), bf16)
            lane = lax.broadcasted_iota(jnp.int32, (64, LANES), 1)
            for r in range(8):
                for part in range(2):
                    for tile in range(TILES):
                        first = GU_ROW * r + FF * part + LANES * tile
                        q, s = first // LANES, first % LANES
                        value = flat[pl.ds(BASE_GU + q, 64, stride=PERIOD), :]
                        if s:
                            after = flat[pl.ds(BASE_GU + q + 1, 64, stride=PERIOD), :]
                            value = jnp.where(
                                lane < LANES - s,
                                pltpu.roll(value, LANES - s, 1),
                                pltpu.roll(after, LANES - s, 1),
                            )
                        if tile == TILES - 1:
                            value = jnp.where(lane < FF - LANES * tile, value, 0.0)
                        gate_up[2 * tile + part, pl.ds(r, 64, stride=8), :] = value
            for k in range(2 * TILES):
                gu_ref[:, 128 * k : 128 * k + 128] = gate_up[k].astype(bf16)

    shapes = [
        ((D, 3 * D), bf16),
        ((D, D), bf16),
        ((D, 2 * FFP), bf16),
        ((FFP, D), bf16),
        ((2, D), f32),
    ]
    return pl.pallas_call(
        body,
        grid=(per_layer,),
        out_shape=[jax.ShapeDtypeStruct(s, d) for s, d in shapes],
        in_specs=[pl.BlockSpec((1, rows, LANES), lambda i: (layer * per_layer + i, 0, 0))],
        out_specs=[pl.BlockSpec(s, lambda i: (0, 0)) for s, _ in shapes],
        scratch_shapes=[pltpu.VMEM((depth, LANES), f32), pltpu.VMEM((2 * TILES, D, LANES), f32)],
        compiler_params=pltpu.CompilerParams(vmem_limit_bytes=60 * MIB),
    )(slots)


def gate_up_segments(q):
    pieces = []
    place_now = LANES * q
    end = place_now + LANES
    while place_now < end:
        r, within = divmod(place_now, GU_ROW)
        part, unit = divmod(within, FF)
        tile, lane_src = divmod(unit, LANES)
        room = min(end - place_now, FF - unit, LANES - lane_src)
        lane_dst = place_now - LANES * q
        pieces.append((r, 2 * tile + part, lane_dst, lane_dst + room, (lane_dst - lane_src) % LANES))
        place_now += room
    return pieces


def weight_grads(a_low, e_lin, ctx, e_attn, b_low, e_both, units, e_ffn, gains, rows, share, per_layer):
    step = chunk_rows(rows)
    depth = LAYER_ROWS + rows

    def body(a_ref, lin_ref, ctx_ref, ea_ref, b_ref, both_ref, u_ref, ef_ref, g_ref, s_ref, flat, gate_up):
        i = pl.program_id(0)

        @pl.when(i == 0)
        def _():
            for t in range(6):
                value = mm_tn(a_ref[...], lin_ref[:, 256 * t : 256 * t + 256])
                for k in range(2):
                    flat[pl.ds(2 * t + k, D, stride=12), :] = value[:, 128 * k : 128 * k + 128]
            for t in range(2):
                value = mm_tn(ctx_ref[...], ea_ref[:, 256 * t : 256 * t + 256])
                for k in range(2):
                    flat[pl.ds(BASE_OUT + 2 * t + k, D, stride=4), :] = value[
                        :, 128 * k : 128 * k + 128
                    ]
                value = mm_tn(u_ref[...], ef_ref[:, 256 * t : 256 * t + 256])
                for k in range(2):
                    flat[pl.ds(BASE_DOWN + 2 * t + k, FF, stride=4), :] = value[
                        0:FF, 128 * k : 128 * k + 128
                    ]
            for t in range(TILES):
                value = mm_tn(b_ref[...], both_ref[:, 256 * t : 256 * t + 256])
                for k in range(2):
                    gate_up[2 * t + k] = value[:, 128 * k : 128 * k + 128]
            for col in range(4):
                flat[pl.ds(BASE_GAINS + col, 2, stride=4), :] = g_ref[:, 128 * col : 128 * col + 128]
            lane = lax.broadcasted_iota(jnp.int32, (64, LANES), 1)
            for q in range(PERIOD):
                value = None
                for r, k, low, high, turn in gate_up_segments(q):
                    piece = gate_up[k, pl.ds(r, 64, stride=8), :]
                    if turn:
                        piece = pltpu.roll(piece, turn, 1)
                    value = piece if value is None else jnp.where(lane < low, value, piece)
                flat[pl.ds(BASE_GU + q, 64, stride=PERIOD), :] = value
            flat[LAYER_ROWS:depth, :] = jnp.zeros((depth - LAYER_ROWS, LANES), f32)

        start = lax.div(share * i, LANES)

        def fill(j, carry):
            s_ref[0, pl.ds(j * step, step), :] = flat[pl.ds(start + j * step, step), :].astype(bf16)
            return carry

        lax.fori_loop(0, rows // step, fill, 0)

    ins = [a_low, e_lin, ctx, e_attn, b_low, e_both, units, e_ffn, gains]
    return pl.pallas_call(
        body,
        grid=(per_layer,),
        out_shape=jax.ShapeDtypeStruct((per_layer, rows, LANES), bf16),
        in_specs=[pl.BlockSpec(v.shape, lambda i: (0, 0)) for v in ins],
        out_specs=pl.BlockSpec((1, rows, LANES), lambda i: (i, 0, 0)),
        scratch_shapes=[pltpu.VMEM((depth, LANES), f32), pltpu.VMEM((2 * TILES, D, LANES), f32)],
        compiler_params=pltpu.CompilerParams(vmem_limit_bytes=60 * MIB),
    )(*ins)


def exchange_keys(kv):
    rows, width = kv.shape
    parts = 4
    piece = rows // parts

    def body(kv_ref, all_ref, send, recv, lsem):
        z, x, y, c = coords()
        bar = pltpu.get_barrier_semaphore()
        to_y = place(z, x, 1 - y, c)
        to_c = place(z, x, y, 1 - c)
        for device in (to_y, to_c):
            pl.semaphore_signal(bar, inc=1, device_id=device, device_id_type=MESH)
        pl.semaphore_wait(bar, 2)
        mine = y * 2 + c
        beyond = (1 - y) * 2 + c
        keep = pltpu.make_async_copy(kv_ref, all_ref.at[mine], lsem)
        keep.start()

        def part(ref, k):
            return ref.at[pl.ds(k * piece, piece)]

        own_y, own_c, pass_c = [], [], []
        for k in range(parts):
            src, dst = part(kv_ref, k), part(all_ref.at[mine], k)
            own_y.append(remote(src, dst, send.at[0, k], recv.at[0, k], to_y))
            own_c.append(remote(src, dst, send.at[1, k], recv.at[1, k], to_c))
            ref = part(all_ref.at[beyond], k)
            pass_c.append(remote(ref, ref, send.at[2, k], recv.at[2, k], to_c))
        for k in range(parts):
            own_y[k].start()
        for k in range(parts):
            own_c[k].start()
        for k in range(parts):
            own_y[k].wait_recv()
            pass_c[k].start()
        for k in range(parts):
            own_c[k].wait_recv()
            pass_c[k].wait_recv()
        for item in own_y + own_c + pass_c:
            item.wait_send()
        keep.wait()

    return pl.pallas_call(
        body,
        out_shape=jax.ShapeDtypeStruct((4, rows, width), kv.dtype),
        in_specs=[vmem_spec()],
        out_specs=vmem_spec(),
        scratch_shapes=[
            pltpu.SemaphoreType.DMA((3, parts)),
            pltpu.SemaphoreType.DMA((3, parts)),
            pltpu.SemaphoreType.DMA,
        ],
        compiler_params=pltpu.CompilerParams(
            collective_id=2, has_side_effects=True, vmem_limit_bytes=32 * MIB
        ),
    )(kv)


def collect_keys(dkv):
    blocks, rows, width = dkv.shape
    parts = 4
    piece = rows // parts

    def body(g_ref, sum_ref, from_c, pair, from_y, send, recv):
        z, x, y, c = coords()
        bar = pltpu.get_barrier_semaphore()
        to_y = place(z, x, 1 - y, c)
        to_c = place(z, x, y, 1 - c)
        for device in (to_y, to_c):
            pl.semaphore_signal(bar, inc=1, device_id=device, device_id_type=MESH)
        pl.semaphore_wait(bar, 2)
        mine = y * 2 + c
        beyond = (1 - y) * 2 + c

        def part(ref, k):
            return ref.at[pl.ds(k * piece, piece)]

        near, wide = [], []
        for h, row in ((0, 1 - y), (1, y)):
            src = g_ref.at[row * 2 + 1 - c]
            near.append(
                [
                    remote(part(src, k), part(from_c.at[h], k), send.at[h, k], recv.at[h, k], to_c)
                    for k in range(parts)
                ]
            )
        for k in range(parts):
            wide.append(remote(part(pair, k), part(from_y, k), send.at[2, k], recv.at[2, k], to_y))
        for group in near:
            for item in group:
                item.start()
        for k in range(parts):
            span = pl.ds(k * piece, piece)
            near[0][k].wait_recv()
            pair[span, :] = (
                from_c[0, span, :].astype(f32) + g_ref[beyond, span, :].astype(f32)
            ).astype(bf16)
            wide[k].start()
        for k in range(parts):
            span = pl.ds(k * piece, piece)
            near[1][k].wait_recv()
            wide[k].wait_recv()
            sum_ref[span, :] = (
                from_c[1, span, :].astype(f32)
                + g_ref[mine, span, :].astype(f32)
                + from_y[span, :].astype(f32)
            ).astype(bf16)
        for item in near[0] + near[1] + wide:
            item.wait_send()

    return pl.pallas_call(
        body,
        out_shape=jax.ShapeDtypeStruct((rows, width), bf16),
        in_specs=[vmem_spec()],
        out_specs=vmem_spec(),
        scratch_shapes=[
            pltpu.VMEM((2, rows, width), bf16),
            pltpu.VMEM((rows, width), bf16),
            pltpu.VMEM((rows, width), bf16),
            pltpu.SemaphoreType.DMA((3, parts)),
            pltpu.SemaphoreType.DMA((3, parts)),
        ],
        compiler_params=pltpu.CompilerParams(
            collective_id=3, has_side_effects=True, vmem_limit_bytes=32 * MIB
        ),
    )(dkv)


def half_swap(u):
    lane = lax.broadcasted_iota(jnp.int32, u.shape, 1)
    return jnp.where(lax.rem(lane, 64) < 32, pltpu.roll(u, 96, 1), pltpu.roll(u, 32, 1))


def project_heads(a_low, w_ref, cos_ref, sin_ref, q_ref, kv_ref):
    for t in range(6):
        lin = mm(a_low, w_ref[:, 256 * t : 256 * t + 256])
        for k in range(2):
            u = lin[:, 128 * k : 128 * k + 128]
            if t < 4:
                u = u * cos_ref[...] + half_swap(u) * sin_ref[...]
            col = 256 * t + 128 * k
            if col < D:
                q_ref[:, col : col + 128] = u.astype(bf16)
            else:
                kv_ref[:, col - D : col - D + 128] = u.astype(bf16)


def norm_factor(r):
    return lax.rsqrt(jnp.mean(r * r, axis=-1, keepdims=True) + NORM_EPS)


def norm_back(e, r, f, g):
    scaled = e * g
    gain = jnp.sum(e * r * f, axis=0, keepdims=True)
    grad = f * scaled - r * (f * f * f) * jnp.mean(scaled * r, axis=-1, keepdims=True)
    return grad, gain


def head_mask(rows, h):
    lane = lax.broadcasted_iota(jnp.int32, (rows, LANES), 1)
    return (lane >= 64) if h else (lane < 64)


def make_bias(bias, length):
    rows, cols = bias.shape
    first = lax.axis_index("sp") * rows
    row = lax.broadcasted_iota(jnp.int32, (rows, cols), 0) + first
    col = lax.broadcasted_iota(jnp.int32, (rows, cols), 1)
    bias[...] = jnp.where((col <= row) & (col < length), 0.0, -1e9)


def attend(q_ref, kv_ref, bias, p_ref, ctx_ref):
    rows = q_ref.shape[0]

    def pair(i, carry):
        span = pl.ds(pl.multiple_of(i * LANES, LANES), LANES)
        vspan = pl.ds(pl.multiple_of(D + i * LANES, LANES), LANES)
        keys = kv_ref[:, span]
        values = kv_ref[:, vspan]
        queries = q_ref[:, span]
        total = jnp.zeros((rows, LANES), f32)
        for h in range(2):
            qm = jnp.where(head_mask(rows, h), queries, jnp.zeros_like(queries))
            vm = jnp.where(head_mask(values.shape[0], h), values, jnp.zeros_like(values))
            logits = mm_nt(qm, keys) * HEAD_DIM ** (-0.5) + bias[...]
            top = jnp.max(logits, axis=-1, keepdims=True)
            soft = jnp.exp(logits - top)
            norm = 1.0 / jnp.sum(soft, axis=-1, keepdims=True)
            low = (soft * norm).astype(bf16)
            p_ref[2 * i + h] = low
            total = total + mm(low, vm)
        ctx_ref[:, span] = total.astype(bf16)
        return carry

    lax.fori_loop(0, HEADS // 2, pair, 0)


def attend_back(q_ref, kv_ref, p_ref, ectx_ref, eq_ref, dkv_ref):
    rows = q_ref.shape[0]
    cols = kv_ref.shape[0]

    def pair(i, carry):
        span = pl.ds(pl.multiple_of(i * LANES, LANES), LANES)
        vspan = pl.ds(pl.multiple_of(D + i * LANES, LANES), LANES)
        keys = kv_ref[:, span]
        values = kv_ref[:, vspan]
        queries = q_ref[:, span]
        grads = ectx_ref[:, span]
        dq = jnp.zeros((rows, LANES), f32)
        dk = jnp.zeros((LANES, cols), f32)
        dv = jnp.zeros((LANES, cols), f32)
        for h in range(2):
            mask = head_mask(rows, h)
            qm = jnp.where(mask, queries, jnp.zeros_like(queries))
            em = jnp.where(mask, grads, jnp.zeros_like(grads))
            km = jnp.where(head_mask(cols, h), keys, jnp.zeros_like(keys))
            low = p_ref[2 * i + h]
            soft = low.astype(f32)
            dp = mm_nt(em, values)
            center = jnp.sum(soft * dp, axis=-1, keepdims=True)
            raw = (soft * (dp - center) * HEAD_DIM ** (-0.5)).astype(bf16)
            dv = dv + mm_tn(em, low)
            dk = dk + mm_tn(qm, raw)
            dq = dq + mm(raw, km)
        eq_ref[:, span] = dq.astype(bf16)
        dkv_ref[:, span] = dk.T.astype(bf16)
        dkv_ref[:, vspan] = dv.T.astype(bf16)
        return carry

    lax.fori_loop(0, HEADS // 2, pair, 0)


def feed_forward(b_low, gu_ref, down_ref, both_ref, units_ref):
    for t in range(TILES):
        both = mm(b_low, gu_ref[:, 256 * t : 256 * t + 256])
        both_ref[:, 256 * t : 256 * t + 256] = both
        gate, up = both[:, :128], both[:, 128:]
        units_ref[:, 128 * t : 128 * t + 128] = (gate / (1.0 + jnp.exp(-gate)) * up).astype(bf16)
    return mm(units_ref[...], down_ref[...])


def feed_back(e_low, gu_ref, down_ref, both_ref, eboth_ref):
    for t in range(TILES):
        eu = mm_nt(e_low, down_ref[128 * t : 128 * t + 128, :])
        gate = both_ref[:, 256 * t : 256 * t + 128]
        up = both_ref[:, 256 * t + 128 : 256 * t + 256]
        sig = 1.0 / (1.0 + jnp.exp(-gate))
        eboth_ref[:, 256 * t : 256 * t + 128] = (eu * up * sig * (1.0 + gate * (1.0 - sig))).astype(bf16)
        eboth_ref[:, 256 * t + 128 : 256 * t + 256] = (eu * gate * sig).astype(bf16)
    return mm_nt(eboth_ref[...], gu_ref[...])


def stage_heads(hidden, w_qkv, cos, sin):
    rows = hidden.shape[0]

    def body(a_ref, w_ref, c_ref, s_ref, q_ref, kv_ref):
        project_heads(a_ref[...], w_ref, c_ref, s_ref, q_ref, kv_ref)

    return local_call(body, [((rows, D), bf16), ((rows, 2 * D), bf16)], [hidden, w_qkv, cos, sin])


def stage_first(length, hidden, q, kv, w_out, w_gu, w_down, gains, next_gains, w_qkv, cos, sin):
    rows = hidden.shape[0]
    cols = kv.shape[0]

    def body(
        l_ref, h_ref, q_ref, kv_ref, wo_ref, gu_ref, dn_ref, g_ref, ng_ref, wq_ref, c_ref, s_ref,
        p_ref, ctx_ref, r1_ref, b_ref, both_ref, units_ref, r2_ref, sec_ref, a1_ref, q1_ref, kv1_ref,
        bias,
    ):
        make_bias(bias, l_ref[0])
        attend(q_ref, kv_ref, bias, p_ref, ctx_ref)
        r1 = h_ref[...].astype(f32) + mm(ctx_ref[...], wo_ref[...])
        r1_ref[...] = r1
        first = r1 * norm_factor(r1) * g_ref[0:1, :]
        b_ref[...] = first.astype(bf16)
        r2 = first + feed_forward(b_ref[...], gu_ref, dn_ref, both_ref, units_ref)
        r2_ref[...] = r2
        second = r2 * norm_factor(r2) * g_ref[1:2, :]
        sec_ref[...] = second
        a1_ref[...] = (second * norm_factor(second) * ng_ref[0:1, :]).astype(bf16)
        project_heads(a1_ref[...], wq_ref, c_ref, s_ref, q1_ref, kv1_ref)

    outs = [
        ((HEADS, rows, cols), bf16),
        ((rows, D), bf16),
        ((rows, D), f32),
        ((rows, D), bf16),
        ((rows, 2 * FFP), f32),
        ((rows, FFP), bf16),
        ((rows, D), f32),
        ((rows, D), f32),
        ((rows, D), bf16),
        ((rows, D), bf16),
        ((rows, 2 * D), bf16),
    ]
    ins = [length, hidden, q, kv, w_out, w_gu, w_down, gains, next_gains, w_qkv, cos, sin]
    return pl.pallas_call(
        body,
        out_shape=[jax.ShapeDtypeStruct(s, d) for s, d in outs],
        in_specs=[pl.BlockSpec(memory_space=pltpu.SMEM)] + [vmem_spec()] * (len(ins) - 1),
        out_specs=[vmem_spec()] * len(outs),
        scratch_shapes=[pltpu.VMEM((rows, cols), f32)],
        compiler_params=pltpu.CompilerParams(vmem_limit_bytes=60 * MIB),
    )(*ins)


def stage_second(length, cotangent, second, q, kv, w_out, w_gu, w_down, gains):
    rows = q.shape[0]
    cols = kv.shape[0]

    def body(
        l_ref, cot_ref, sec_ref, q_ref, kv_ref, wo_ref, gu_ref, dn_ref, g_ref,
        o_ref, ctx_ref, b_ref, units_ref, eboth_ref, ef_ref, ea_ref, e3_ref, eq_ref, dkv_ref, gg_ref,
        bias, p_ref, both_ref, ectx_ref,
    ):
        length_now = l_ref[0]
        make_bias(bias, length_now)
        attend(q_ref, kv_ref, bias, p_ref, ctx_ref)
        third = sec_ref[...] + mm(ctx_ref[...], wo_ref[...])
        f4 = norm_factor(third)
        b_ref[...] = (third * f4 * g_ref[1:2, :]).astype(bf16)
        o_ref[...] = third + feed_forward(b_ref[...], gu_ref, dn_ref, both_ref, units_ref)
        place_now = lax.broadcasted_iota(jnp.int32, (rows, D), 0) + lax.axis_index("sp") * rows
        e_out = jnp.where(place_now < length_now, cot_ref[...], 0.0)
        ef_ref[...] = e_out.astype(bf16)
        e_b = feed_back(ef_ref[...], gu_ref, dn_ref, both_ref, eboth_ref)
        grad, gain = norm_back(e_b, third, f4, g_ref[1:2, :])
        gg_ref[...] = gain
        e3 = e_out + grad
        e3_ref[...] = e3
        ea_ref[...] = e3.astype(bf16)
        ectx_ref[...] = mm_nt(ea_ref[...], wo_ref[...]).astype(bf16)
        attend_back(q_ref, kv_ref, p_ref, ectx_ref, eq_ref, dkv_ref)

    outs = [
        ((rows, D), f32),
        ((rows, D), bf16),
        ((rows, D), bf16),
        ((rows, FFP), bf16),
        ((rows, 2 * FFP), bf16),
        ((rows, D), bf16),
        ((rows, D), bf16),
        ((rows, D), f32),
        ((rows, D), bf16),
        ((cols, 2 * D), bf16),
        ((1, D), f32),
    ]
    ins = [length, cotangent, second, q, kv, w_out, w_gu, w_down, gains]
    return pl.pallas_call(
        body,
        out_shape=[jax.ShapeDtypeStruct(s, d) for s, d in outs],
        in_specs=[pl.BlockSpec(memory_space=pltpu.SMEM)] + [vmem_spec()] * (len(ins) - 1),
        out_specs=[vmem_spec()] * len(outs),
        scratch_shapes=[
            pltpu.VMEM((rows, cols), f32),
            pltpu.VMEM((HEADS, rows, cols), bf16),
            pltpu.VMEM((rows, 2 * FFP), f32),
            pltpu.VMEM((rows, D), bf16),
        ],
        compiler_params=pltpu.CompilerParams(vmem_limit_bytes=60 * MIB),
    )(*ins)


def lin_grads(eq_ref, ekv_ref, cos_ref, sin_ref, lin_ref):
    for t in range(12):
        col = 128 * t
        src = eq_ref[:, col : col + 128] if t < 4 else ekv_ref[:, col - D : col - D + 128]
        if t < 8:
            w = src.astype(f32)
            src = (w * cos_ref[...] - half_swap(w) * sin_ref[...]).astype(bf16)
        lin_ref[:, col : col + 128] = src


def stage_back(
    e_q, e_kv, e3, second, next_gains, w_qkv, cos, sin,
    r1, r2, both, gains, w_gu, w_down, w_out, q, kv, p,
):
    rows = e_q.shape[0]
    cols = kv.shape[0]

    def body(
        eq_ref, ekv_ref, e3_ref, sec_ref, ng_ref, wq_ref, c_ref, s_ref,
        r1_ref, r2_ref, both_ref, g_ref, gu_ref, dn_ref, wo_ref, q_ref, kv_ref, p_ref,
        lin_ref, eboth_ref, ef_ref, ea_ref, e1_ref, eq0_ref, dkv_ref, gg_ref,
        ectx_ref,
    ):
        lin_grads(eq_ref, ekv_ref, c_ref, s_ref, lin_ref)
        e_a = mm_nt(lin_ref[...], wq_ref[...])
        second = sec_ref[...]
        grad, gain3 = norm_back(e_a, second, norm_factor(second), ng_ref[0:1, :])
        e2 = e3_ref[...] + grad
        r2 = r2_ref[...]
        er2, gain2 = norm_back(e2, r2, norm_factor(r2), g_ref[1:2, :])
        ef_ref[...] = er2.astype(bf16)
        e_first = er2 + feed_back(ef_ref[...], gu_ref, dn_ref, both_ref, eboth_ref)
        r1 = r1_ref[...]
        er1, gain1 = norm_back(e_first, r1, norm_factor(r1), g_ref[0:1, :])
        e1_ref[...] = er1
        ea_ref[...] = er1.astype(bf16)
        gg_ref[0:1, :] = gain1
        gg_ref[1:2, :] = gain2
        gg_ref[2:3, :] = gain3
        ectx_ref[...] = mm_nt(ea_ref[...], wo_ref[...]).astype(bf16)
        attend_back(q_ref, kv_ref, p_ref, ectx_ref, eq0_ref, dkv_ref)

    return local_call(
        body,
        [
            ((rows, 3 * D), bf16),
            ((rows, 2 * FFP), bf16),
            ((rows, D), bf16),
            ((rows, D), bf16),
            ((rows, D), f32),
            ((rows, D), bf16),
            ((cols, 2 * D), bf16),
            ((3, D), f32),
        ],
        [
            e_q, e_kv, e3, second, next_gains, w_qkv, cos, sin,
            r1, r2, both, gains, w_gu, w_down, w_out, q, kv, p,
        ],
        [pltpu.VMEM((rows, D), bf16)],
    )


def stage_end(e_q, e_kv, e1, w_qkv, cos, sin):
    rows = e_q.shape[0]

    def body(eq_ref, ekv_ref, e1_ref, wq_ref, c_ref, s_ref, lin_ref, o_ref):
        lin_grads(eq_ref, ekv_ref, c_ref, s_ref, lin_ref)
        o_ref[...] = e1_ref[...] + mm_nt(lin_ref[...], wq_ref[...])

    return local_call(
        body, [((rows, 3 * D), bf16), ((rows, D), f32)], [e_q, e_kv, e1, w_qkv, cos, sin]
    )


def reduce_and_update(slots_zero, slots_one, gains_part, master, one, two, zn, rows, share):
    half = rows // 2
    step = chunk_rows(rows)
    ndev = zn * 8
    per_layer = ndev // 2
    turns = rows // step

    def body(
        g0_ref, g1_ref, gp_ref, m_ref, one_ref, two_ref,
        nm_ref, n1_ref, n2_ref, gn_ref, gg_ref,
        acc, rc, rd, rx, ry, rz, fin, sq, sqs, gps, send, recv, lsem, ssem, rsem,
    ):
        z, x, y, c = coords()
        me = ((z * 2 + x) * 2 + y) * 2 + c
        bar = pltpu.get_barrier_semaphore()

        def peer(d):
            tgt = lax.rem(me + d, ndev)
            return {"dp": lax.div(tgt, 4), "sp": lax.rem(tgt, 4)}

        def hello(d, carry):
            pl.semaphore_signal(bar, inc=1, device_id=peer(d), device_id_type=MESH)
            return carry

        lax.fori_loop(1, ndev, hello, 0)

        to_x = place(z, 1 - x, y, c)
        to_y = place(z, x, 1 - y, c)
        to_c = place(z, x, y, 1 - c)
        spots = [(x, y), (1 - x, y), (x, 1 - y), (1 - x, 1 - y)]

        def slot(zp, rel, cp):
            xp, yp = spots[rel]
            return ((zp * 2 + xp) * 2 + yp) * 2 + cp

        def on_source(zp, rel, cp, act):
            index = slot(zp, rel, cp)

            @pl.when(index < per_layer)
            def _():
                act(g0_ref.at[index])

            @pl.when(index >= per_layer)
            def _():
                act(g1_ref.at[index - per_layer])

        def cp(src, dst, zp, s, r, device):
            return remote(src, dst, send.at[zp, s], recv.at[zp, r], device)

        def core_send(zp, rel, src):
            return cp(src, rc.at[zp, rel], zp, rel, rel, to_c)

        def load(zp, rel, src):
            return pltpu.make_async_copy(src, acc.at[zp, rel], lsem.at[zp, rel])

        def diag_a(zp):
            return cp(acc.at[zp, 3, pl.ds(0, half)], rd.at[zp, pl.ds(0, half)], zp, 4, 4, to_y)

        def diag_b(zp):
            return cp(acc.at[zp, 3, pl.ds(half, half)], rd.at[zp, pl.ds(half, half)], zp, 5, 5, to_x)

        def send_x(zp):
            return cp(acc.at[zp, 1], rx.at[zp], zp, 6, 6, to_x)

        def send_y(zp):
            return cp(acc.at[zp, 2], ry.at[zp], zp, 7, 7, to_y)

        def right(zp):
            return cp(acc.at[zp, 0], rz.at[zp, 0], zp, 8, 8, place(z + 1, x, y, c))

        def left(zp):
            return cp(acc.at[zp, 0], rz.at[zp, 1], zp, 8, 9, place(z - 1, x, y, c))

        def add_into(dst, low, high, *srcs):
            size = step if (high - low) % step == 0 else 16

            def one_step(i, carry):
                span = pl.ds(pl.multiple_of(low + i * size, 16), size)
                value = dst[span, :].astype(f32)
                for src in srcs:
                    value = value + src[span, :].astype(f32)
                dst[span, :] = value.astype(bf16)
                return carry

            lax.fori_loop(0, (high - low) // size, one_step, 0)

        def valid(k):
            zp = order_at(2 * zn - 2 - k, z)
            return zp, (k >= 0) & (k < 2 * zn - 1) & (zp >= 0) & (zp < zn)

        def stage_c(k):
            zp, ok = valid(k)

            @pl.when(ok)
            def _():
                for rel in (3, 1, 2, 0):
                    on_source(zp, rel, 1 - c, lambda src, rel=rel: core_send(zp, rel, src).start())
                    on_source(zp, rel, c, lambda src, rel=rel: load(zp, rel, src).start())

        def stage_one(k):
            zp, ok = valid(k)

            @pl.when(ok)
            def _():
                for rel in (3, 1, 2, 0):
                    core_send(zp, rel, g0_ref.at[0]).wait_recv()
                    load(zp, rel, g0_ref.at[0]).wait()
                    add_into(acc.at[zp, rel], 0, rows, rc.at[zp, rel])
                    if rel == 3:
                        diag_a(zp).start()
                        diag_b(zp).start()

        def stage_two(k):
            zp, ok = valid(k)

            @pl.when(ok)
            def _():
                diag_a(zp).wait_recv()
                add_into(acc.at[zp, 1], 0, half, rd.at[zp])
                send_x(zp).start()
                diag_b(zp).wait_recv()
                add_into(acc.at[zp, 2], half, rows, rd.at[zp])
                send_y(zp).start()

        def stage_three(k):
            zp, ok = valid(k)

            @pl.when(ok & (zp != z))
            def _():
                send_x(zp).wait_recv()
                send_y(zp).wait_recv()
                add_into(acc.at[zp, 0], 0, rows, rx.at[zp], ry.at[zp])

                @pl.when((zp > z) & (z > 0))
                def _():
                    right(zp).wait_recv()
                    add_into(acc.at[zp, 0], 0, rows, rz.at[zp, 0])

                @pl.when((zp < z) & (z < zn - 1))
                def _():
                    left(zp).wait_recv()
                    add_into(acc.at[zp, 0], 0, rows, rz.at[zp, 1])

                pl.when(zp > z)(lambda: right(zp).start())
                pl.when(zp < z)(lambda: left(zp).start())

        pl.semaphore_wait(bar, ndev - 1)

        def tell(src, dst, s):
            def go(d, carry):
                remote(src, dst.at[me], ssem.at[s], rsem.at[s], peer(d)).start()
                return carry

            lax.fori_loop(1, ndev, go, 0)

        def hear(dst, s):
            part = dst.at[pl.ds(0, ndev - 1)]
            both = remote(part, part, ssem.at[s], rsem.at[s], to_c)
            both.wait_send()
            both.wait_recv()

        for k in range(3):
            stage_c(k)
        tell(gp_ref, gps, 0)
        gps[me] = gp_ref[...]

        def turn(k, carry):
            stage_one(k)
            stage_c(k + 3)
            stage_two(k - 1)
            stage_three(k - 2)
            return carry

        lax.fori_loop(0, 2 * zn + 1, turn, 0)

        send_x(z).wait_recv()
        send_y(z).wait_recv()
        pl.when(z > 0)(lambda: right(z).wait_recv())
        pl.when(z < zn - 1)(lambda: left(z).wait_recv())

        def total(i, carry):
            span = pl.ds(pl.multiple_of(i * step, 16), step)
            value = (
                acc[z, 0, span, :].astype(f32)
                + rx[z, span, :].astype(f32)
                + ry[z, span, :].astype(f32)
            )
            value = value + jnp.where(z > 0, rz[z, 0, span, :].astype(f32), 0.0)
            value = value + jnp.where(z < zn - 1, rz[z, 1, span, :].astype(f32), 0.0)
            fin[span, :] = value
            return carry

        lax.fori_loop(0, turns, total, 0)
        fin[pl.ds(rows, 8), :] = jnp.zeros((8, LANES), f32)

        shift = lax.rem(share * me, LANES)
        back = lax.rem(LANES - shift, LANES)
        lane = lax.broadcasted_iota(jnp.int32, (step, LANES), 1)
        row = lax.broadcasted_iota(jnp.int32, (step, LANES), 0)

        def realign(i, carry):
            now = pltpu.roll(fin[pl.ds(i * step, step), :], back, 1)
            after = pltpu.roll(fin[pl.ds(i * step + 1, step), :], back, 1)
            value = jnp.where(lane < LANES - shift, now, after)
            value = jnp.where((row + i * step) * LANES + lane < share, value, 0.0)
            n1_ref[pl.ds(i * step, step), :] = value
            square = value * value
            return carry + jnp.sum(square.reshape(step // 8, 8, LANES), axis=0)

        sq[...] = lax.fori_loop(0, turns, realign, jnp.zeros((8, LANES), f32))
        tell(sq, sqs, 1)
        sqs[me] = sq[...]

        def finish(i, carry):
            for rel in range(4):
                core_send(i, rel, g0_ref.at[0]).wait_send()
            for item in (diag_a(i), diag_b(i), send_x(i), send_y(i)):
                item.wait_send()
            pl.when(i > z)(lambda: right(i).wait_send())
            pl.when(i < z)(lambda: left(i).wait_send())
            return carry

        lax.fori_loop(0, zn, finish, 0)
        hear(gps, 0)
        gg_ref[...] = lax.fori_loop(
            1, ndev, lambda i, s: s + gps[i], gps[0]
        )
        hear(sqs, 1)
        squares = lax.fori_loop(1, ndev, lambda i, s: s + sqs[i], sqs[0])
        norm = jnp.sqrt(jnp.sum(squares, keepdims=True))
        gn_ref[...] = jnp.broadcast_to(norm, (8, LANES))
        scale = jnp.minimum(1.0, 1.0 / norm)
        correction = 1.0 - 0.5**STEP

        def update(i, carry):
            span = pl.ds(pl.multiple_of(i * step, 16), step)
            clipped = n1_ref[span, :] * scale
            new_one = 0.5 * one_ref[span, :] + 0.5 * clipped
            new_two = 0.5 * two_ref[span, :] + 0.5 * clipped * clipped
            n1_ref[span, :] = new_one
            n2_ref[span, :] = new_two
            nm_ref[span, :] = m_ref[pl.ds(8 + i * step, step), :] * (
                1.0 - LEARN_RATE * DECAY_RATE
            ) - LEARN_RATE * (new_one / correction) / (jnp.sqrt(new_two / correction) + ADAM_EPS)
            return carry

        lax.fori_loop(0, turns, update, 0)

    flat = jax.ShapeDtypeStruct((rows, LANES), f32)
    return pl.pallas_call(
        body,
        out_shape=[
            flat,
            flat,
            flat,
            jax.ShapeDtypeStruct((8, LANES), f32),
            jax.ShapeDtypeStruct((16, LANES), f32),
        ],
        in_specs=[any_spec(), any_spec()] + [vmem_spec()] * 4,
        out_specs=[vmem_spec()] * 5,
        scratch_shapes=[
            pltpu.VMEM((zn, 4, rows, LANES), bf16),
            pltpu.VMEM((zn, 4, rows, LANES), bf16),
            pltpu.VMEM((zn, rows, LANES), bf16),
            pltpu.VMEM((zn, rows, LANES), bf16),
            pltpu.VMEM((zn, rows, LANES), bf16),
            pltpu.VMEM((zn, 2, rows, LANES), bf16),
            pltpu.VMEM((rows + 8, LANES), f32),
            pltpu.VMEM((8, LANES), f32),
            pltpu.VMEM((ndev, 8, LANES), f32),
            pltpu.VMEM((ndev, 16, LANES), f32),
            pltpu.SemaphoreType.DMA((zn, 9)),
            pltpu.SemaphoreType.DMA((zn, 10)),
            pltpu.SemaphoreType.DMA((zn, 4)),
            pltpu.SemaphoreType.DMA((2,)),
            pltpu.SemaphoreType.DMA((2,)),
        ],
        compiler_params=pltpu.CompilerParams(
            collective_id=4, has_side_effects=True, vmem_limit_bytes=60 * MIB
        ),
    )(slots_zero, slots_one, gains_part, master, one, two)


def rope_rows(rows):
    frequency = jnp.exp(
        -jnp.log(10000.0) * jnp.arange(HEAD_DIM // 2).astype(f32) * 2.0 / HEAD_DIM
    )
    positions = lax.axis_index("sp") * rows + jnp.arange(rows)
    angles = positions.astype(f32)[:, None] * frequency[None, :]
    cos = jnp.cos(angles)
    sin = jnp.sin(angles)
    return (
        jnp.concatenate([cos] * 4, axis=1),
        jnp.concatenate([-sin, sin, -sin, sin], axis=1),
    )


def step_shard(dp_size, sp_size, hidden_in, cotangent, lengths, master, moment_one, moment_two):
    share = master.shape[0]
    zn = dp_size // 2
    per_layer = dp_size * sp_size // 2
    rows = -(-(-(-share // LANES) + 1) // 32) * 32
    seqs, tokens, width = hidden_in.shape

    def pad(flat, lead):
        return jnp.pad(flat, (lead * LANES, rows * LANES - share)).reshape(rows + lead, LANES)

    master_pad = pad(master, 8)
    slots = gather_weights(master_pad, zn, rows, share, 0, zn)
    wq0, wo0, wg0, wd0, g0 = unpack_weights(slots, 0, rows, share)
    wq1, wo1, wg1, wd1, g1 = unpack_weights(slots, 1, rows, share)
    cos, sin = rope_rows(tokens)
    hidden = hidden_in.reshape(tokens, width)

    def join(kv):
        return exchange_keys(kv).reshape(4 * tokens, 2 * width)

    def collect(dkv):
        return collect_keys(dkv.reshape(4, tokens, 2 * width))

    q0, kv0 = stage_heads(hidden, wq0, cos, sin)
    kv0 = join(kv0)
    p0, ctx0, r1, b0, both0, units0, r2, second, a1, q1, kv1 = stage_first(
        lengths, hidden, q0, kv0, wo0, wg0, wd0, g0, g1, wq1, cos, sin
    )
    kv1 = join(kv1)
    output, ctx1, b1, units1, eboth1, ef1, ea1, e3, eq1, dkv1, gain4 = stage_second(
        lengths, cotangent.reshape(tokens, width), second, q1, kv1, wo1, wg1, wd1, g1
    )
    ekv1 = collect(dkv1)
    lin1, eboth0, ef0, ea0, e1, eq0, dkv0, gains3 = stage_back(
        eq1, ekv1, e3, second, g1, wq1, cos, sin, r1, r2, both0, g0, wg0, wd0, wo0, q0, kv0, p0
    )
    gains_one = jnp.concatenate([gains3[2:3], gain4], axis=0)
    grads_one = weight_grads(
        a1, lin1, ctx1, ea1, b1, eboth1, units1, ef1, gains_one, rows, share, per_layer
    )
    ekv0 = collect(dkv0)
    lin0, input_grad = stage_end(eq0, ekv0, e1, wq0, cos, sin)
    gains_zero = gains3[0:2]
    grads_zero = weight_grads(
        hidden, lin0, ctx0, ea0, b0, eboth0, units0, ef0, gains_zero, rows, share, per_layer
    )
    gains_part = jnp.concatenate([gains_zero, gains_one], axis=0).reshape(16, LANES)
    new_master, new_one, new_two, norm, gains = reduce_and_update(
        grads_zero, grads_one, gains_part, master_pad, pad(moment_one, 0), pad(moment_two, 0),
        zn, rows, share,
    )

    def flat(value):
        return value.reshape(-1)[:share]

    new_master = flat(new_master)
    return (
        output.reshape(hidden_in.shape),
        input_grad.reshape(hidden_in.shape),
        new_master,
        flat(new_one),
        flat(new_two),
        new_master.astype(bf16),
        norm[0, 0],
        gains.reshape(2, 2, width),
    )


def solution(mesh):
    in_specs = (
        P("dp", "sp", None),
        P("dp", "sp", None),
        P("dp"),
        P(("dp", "sp")),
        P(("dp", "sp")),
        P(("dp", "sp")),
    )
    out_specs = (
        P("dp", "sp", None),
        P("dp", "sp", None),
        P(("dp", "sp")),
        P(("dp", "sp")),
        P(("dp", "sp")),
        P(("dp", "sp")),
        P(),
        P(),
    )
    body = functools.partial(step_shard, mesh.shape["dp"], mesh.shape["sp"])
    return jax.shard_map(body, mesh=mesh, in_specs=in_specs, out_specs=out_specs, check_vma=False)
```

time: 1100 us -> 354 us (0.32)
  waiting for transfers between devices: 548 us -> 0 us
  Pallas kernels: 0 us -> 326 us
  local copies, waits for them, and re-layouts: 212 us -> 20.7 us
  matrix products: 180 us -> 0 us
  blocking collectives: 62.5 us -> 0 us
  other arithmetic: 48.7 us -> 5.18 us
  starting transfers between devices: 25.3 us -> 0 us
  between operations: 17.7 us -> 1.48 us
    unnamed x6 -> x0, waiting for transfers between devices: 542 us -> none
    pallas_call x0 -> x15, Pallas kernels: none -> 326 us  [the longest x1 80 us: reduce_and_update(): pl.pallas_call(body, out_shape=[flat, flat, flat, jax.ShapeDtypeStruct((8...]
    dot_general x48 -> x0, matrix products: 180 us -> none  [the longest x4 50.6 us: attend_backward(): jnp.einsum('hqk,qhd->khd', score_grad, query_block, preferred_element_typ...]
    convert_element_type x5 -> x0, local copies, waits for them, and re-layouts: 44.6 us -> none  [the longest x2 35.1 us: shards(): grad_grid.astype(jnp.bfloat16)]
    reshape x12 -> x4, local copies, waits for them, and re-layouts: 47 us -> 3.78 us  [the longest x2 2.56 us: pad(): jnp.pad(flat, (lead * LANES, rows * LANES - share))]
    slice x23 -> x5, local copies, waits for them, and re-layouts: 43.5 us -> 4.35 us  [the longest x2 1.87 us: flat(): return value.reshape(-1)[:share]]
    psum x1 -> x0, blocking collectives: 39 us -> none  [shards(): lax.psum((jnp.sum(grad_shard * grad_shard), gains_local), ('dp', 'sp'))]
    unnamed x133 -> x34, local copies, waits for them, and re-layouts: 40.6 us -> 12.6 us
  transfers between devices with their start and end apart: 9 -> 0, of which waited for: 5 -> 0; matrix products, arithmetic and copies ran while one was open for 9% -> 0% of each run, Pallas kernels for 0% -> 0%
where the time goes in v1:
time: 354 us; the launch traced here: 353 us
  Pallas kernels  326 us (92%)
  local copies, waits for them, and re-layouts  20.7 us (6%)
  other arithmetic  5.18 us (1%)
    pallas_call x1, Pallas kernels, reduce_and_update(): pl.pallas_call(body, out_shape=[flat, flat, flat, jax.ShapeDtypeStruct((8...  80 us
    pallas_call x1, Pallas kernels, gather_weights(): pl.pallas_call(body, out_shape=jax.ShapeDtypeStruct((nz * 8, rows, LANES)...  65.1 us
    pallas_call x2, Pallas kernels, unpack_weights(): pl.pallas_call(body, grid=(per_layer,), out_shape=[jax.ShapeDtypeStruct(s...  31.7 us
    pallas_call x2, Pallas kernels, collect_keys(): pl.pallas_call(body, out_shape=jax.ShapeDtypeStruct((rows, width), bf16),...  31.6 us
    pallas_call x2, Pallas kernels, exchange_keys(): pl.pallas_call(body, out_shape=jax.ShapeDtypeStruct((4, rows, width), kv....  31.1 us
    pallas_call x2, Pallas kernels, weight_grads(): pl.pallas_call(body, grid=(per_layer,), out_shape=jax.ShapeDtypeStruct((p...  27.8 us
    pallas_call x3, Pallas kernels, local_call(): pl.pallas_call(body, out_shape=[jax.ShapeDtypeStruct(s, d) for s, d in ou...  23.5 us
    pallas_call x1, Pallas kernels, stage_second(): pl.pallas_call(body, out_shape=[jax.ShapeDtypeStruct(s, d) for s, d in ou...  20.4 us

profile of v1, /device:TPU:0, one launch (start us, length us, event | category | flops | bytes accessed | tf_op | source)
XLA Modules:
  0.0 353.3 jit_solution(7811752039005960122)
XLA Ops:
  2.2 1.2 pad_bitcast_fusion.x_ref.m_ref
  3.4 65.1 %shard_map.125.s_ref = bf16[32,1568,128]{2,1,0:T(8,128)(2,1)S(1)} custom-call(f32[1576,128]{1,0:T(8,128)S(1)} %pad_bitcast_fusion.x_ref.m_ref), custom_call_target="tpu_custom_call" | custom-call | tf_op jit(solution)/shard_map/pallas_call | solution.py:250
  68.5 4.6 %copy-done = bf16[32,1568,128]{2,1,0:T(8,128)(2,1)} copy-done((bf16[32,1568,128]{2,1,0:T(8,128)(2,1)}, bf16[32,1568,128]{2,1,0:T(8,128)(2,1)S(1)}, u32[]{:S(2)}) %copy-start) | copy-done | bytes 12845080
  73.1 15.8 %shard_map.126 = (bf16[512,1536]{1,0:T(8,128)(2,1)}, bf16[512,512]{1,0:T(8,128)(2,1)}, bf16[512,2816]{1,0:T(8,128)(2,1)}, bf16[1408,512]{1,0:T(8,128)(2,1)}, f32[2,512]{1,0:T(2,128)}) custom-call(bf16[32,1568,128]{2,1,0:T(8,128)(2,1)} %copy-done), custom_call_target="tpu_custom_call" | custom-call | tf_op jit(solution)/shard_map/pallas_call | solution.py:332
  88.9 3.2 shard_map.127
  92.1 1.0 copy-done.9
  93.1 15.4 %shard_map.128 = bf16[4,256,1024]{2,1,0:T(8,128)(2,1)S(1)} custom-call(bf16[256,1024]{1,0:T(8,128)(2,1)S(1)} %copy-done.9), custom_call_target="tpu_custom_call" | custom-call | tf_op jit(solution)/shard_map/pallas_call | solution.py:461
  108.6 1.3 copy-done.1
  109.9 15.9 %shard_map.129 = (bf16[512,1536]{1,0:T(8,128)(2,1)}, bf16[512,512]{1,0:T(8,128)(2,1)}, bf16[512,2816]{1,0:T(8,128)(2,1)}, bf16[1408,512]{1,0:T(8,128)(2,1)}, f32[2,512]{1,0:T(2,128)}) custom-call(bf16[32,1568,128]{2,1,0:T(8,128)(2,1)} %copy-done), custom_call_target="tpu_custom_call" | custom-call | tf_op jit(solution)/shard_map/pallas_call | solution.py:332
  126.4 14.9 %shard_map.130 = (bf16[8,256,1024]{2,1,0:T(8,128)(2,1)}, bf16[256,512]{1,0:T(8,128)(2,1)}, f32[256,512]{1,0:T(8,128)}, bf16[256,512]{1,0:T(8,128)(2,1)}, f32[256...) custom-call(s32[1]{0:T(128)S(6)} %copy.15.l_ref, ...), custom_call_target="tpu_custom_call" | custom-call | tf_op jit(solution)/shard_map/pallas_call | solution.py:716
  142.4 15.6 %shard_map.131 = bf16[4,256,1024]{2,1,0:T(8,128)(2,1)S(1)} custom-call(bf16[256,1024]{1,0:T(8,128)(2,1)S(1)} %copy-done.8), custom_call_target="tpu_custom_call" | custom-call | tf_op jit(solution)/shard_map/pallas_call | solution.py:461
  158.0 1.4 copy-done.2
  159.4 20.4 %shard_map.132 = (f32[256,512]{1,0:T(8,128)}, bf16[256,512]{1,0:T(8,128)(2,1)}, bf16[256,512]{1,0:T(8,128)(2,1)}, bf16[256,1408]{1,0:T(8,128)(2,1)}, bf16[256,28...) custom-call(s32[1]{0:T(128)S(6)} %copy.15.l_ref, ...), custom_call_target="tpu_custom_call" | custom-call | tf_op jit(solution)/shard_map/pallas_call | solution.py:768
  179.8 1.6 copy-done.6
  181.3 15.8 %shard_map.133.ekv_ref = bf16[256,1024]{1,0:T(8,128)(2,1)S(1)} custom-call(bf16[4,256,1024]{2,1,0:T(8,128)(2,1)S(1)} %bitcast.22), custom_call_target="tpu_custom_call" | custom-call | tf_op jit(solution)/shard_map/pallas_call | solution.py:529
  197.9 17.0 %shard_map.134 = (bf16[256,1536]{1,0:T(8,128)(2,1)}, bf16[256,2816]{1,0:T(8,128)(2,1)}, bf16[256,512]{1,0:T(8,128)(2,1)}, bf16[256,512]{1,0:T(8,128)(2,1)}, f32[...) custom-call(bf16[256,512]{1,0:T(8,128)(2,1)} %get-tuple-element.73.eq_ref, ...), custom_call_target="tpu_custom_call" | custom-call | tf_op jit(solution)/shard_map/pallas_call | solution.py:62
  217.6 13.9 %shard_map.138.g1_ref = bf16[16,1568,128]{2,1,0:T(8,128)(2,1)} custom-call(bf16[256,512]{1,0:T(8,128)(2,1)} %get-tuple-element.92.a_ref, bf16[256,1536]{1,0:T(8,128)(2,1)} %get-tuple-element.93.lin_ref, bf16[256,512]{1,0:T(8,128)(2,1)} %get-tuple-element.94.ctx_ref, bf16[256,512]{1,0:T(8,128)(2,1)} %get-tuple-element.95.ea_ref, ...), custom_call_target="tpu_custom_call" | custom-call | tf_op jit(solution)/shard_map/pallas_call | solution.py:408
  231.5 15.8 %shard_map.135.ekv_ref = bf16[256,1024]{1,0:T(8,128)(2,1)S(1)} custom-call(bf16[4,256,1024]{2,1,0:T(8,128)(2,1)S(1)} %bitcast.21), custom_call_target="tpu_custom_call" | custom-call | tf_op jit(solution)/shard_map/pallas_call | solution.py:529
  248.0 3.4 shard_map.136
  252.0 13.9 %shard_map.137.g0_ref = bf16[16,1568,128]{2,1,0:T(8,128)(2,1)} custom-call(bf16[256,512]{1,0:T(8,128)(2,1)} %bitcast.25, bf16[256,1536]{1,0:T(8,128)(2,1)} %get-tuple-element.84.lin_ref, bf16[256,512]{1,0:T(8,128)(2,1)} %get-tuple-element.85.ctx_ref, bf16[256,512]{1,0:T(8,128)(2,1)} %get-tuple-element.86.ea_ref, bf16[256,512]{1,0:T(8,128)(2,1)} %get-tuple-element.87.b_ref, ...), custom_call_target="tpu_custom_call" | custom-call | tf_op jit(solution)/shard_map/pallas_call | solution.py:408
  265.9 1.4 pad_bitcast_fusion.1
  267.3 80.0 %shard_map.139 = (f32[1568,128]{1,0:T(8,128)}, f32[1568,128]{1,0:T(8,128)}, f32[1568,128]{1,0:T(8,128)}, f32[8,128]{1,0:T(8,128)}, f32[16,128]{1,0:T(8,128)}) custom-call(bf16[16,1568,128]{2,1,0:T(8,128)(2,1)} %shard_map.137.g0_ref, bf16[16,1568,128]{2,1,0:T(8,128)(2,1)} %shard_map.138.g1_ref, f32[16,128]{1,0:T(8,128)} %reshape.84.gp_ref, ...), custom_call_target="tpu_custom_call" | custom-call | tf_op jit(solution)/shard_map/pallas_call | solution.py:1106
  347.3 2.3 fusion.1
  352.1 1.2 slice.24
  (41 shorter events, 9.9 us)
Async XLA Ops:
  3.4 65.1 %copy-start.3 = (f32[1576,128]{1,0:T(8,128)}, f32[1576,128]{1,0:T(8,128)S(1)}, u32[]{:S(2)}) copy-start(f32[1576,128]{1,0:T(8,128)S(1)} %pad_bitcast_fusion.x_ref.m_ref) | copy-start | bytes 2420740
  68.5 4.6 %copy-start = (bf16[32,1568,128]{2,1,0:T(8,128)(2,1)}, bf16[32,1568,128]{2,1,0:T(8,128)(2,1)S(1)}, u32[]{:S(2)}) copy-start(bf16[32,1568,128]{2,1,0:T(8,128)(2,1)S(1)} %shard_map.125.s_ref) | copy-start | bytes 38535172
  92.1 1.0 copy-start.9
  108.6 1.3 copy-start.1
  141.3 1.0 copy-start.8
  158.0 1.4 copy-start.2
  179.8 1.6 copy-start.6
  197.1 0.8 copy-start.4
  197.9 17.0 %copy-start.16 = (f32[1,512]{1,0:T(1,128)S(1)}, f32[1,512]{1,0:T(1,128)}, u32[]{:S(2)}) copy-start(f32[1,512]{1,0:T(1,128)} %get-tuple-element.100) | copy-start | bytes 6148
  217.6 13.9 %copy-start.5 = (bf16[1024,1024]{1,0:T(8,128)(2,1)S(1)}, bf16[1024,1024]{1,0:T(8,128)(2,1)}, u32[]{:S(2)}) copy-start(bf16[1024,1024]{1,0:T(8,128)(2,1)} %get-tuple-element.81) | copy-start | bytes 6291460
  247.2 0.8 copy-start.7
  248.0 3.4 copy-start.14
  252.0 13.9 %copy-start.10 = (f32[196928]{0:T(1024)S(1)}, f32[196928]{0:T(1024)}, u32[]{:S(2)}) copy-start(f32[196928]{0:T(1024)} %param.11) | copy-start | bytes 2363140
  252.0 13.9 %copy-start.11 = (f32[196928]{0:T(1024)S(1)}, f32[196928]{0:T(1024)}, u32[]{:S(2)}) copy-start(f32[196928]{0:T(1024)} %param.10) | copy-start | bytes 2363140
  347.3 2.4 copy-start.13
  347.3 3.3 copy-start.12
  347.3 4.2 %copy-start.15 = (f32[16,128]{1,0:T(8,128)S(1)}, f32[16,128]{1,0:T(8,128)}, u32[]{:S(2)}) copy-start(f32[16,128]{1,0:T(8,128)} %get-tuple-element.105) | copy-start | bytes 24580

commit v2 on v1

--- a/solution.py
+++ b/solution.py
@@ -95,189 +95,206 @@
     return z + jnp.where(lax.rem(tau, 2) == 1, -step, step)
 
 
-def gather_weights(master_pad, zn, rows, share, zlo, zhi):
-    nz = zhi - zlo
-    half = rows // 2
-    step = chunk_rows(rows)
-
-    def body(x_ref, out_ref, own, send, recv, lsem):
+class Gather:
+    def __init__(self, out_ref, own, send, recv, zn, rows, zlo, zhi):
+        self.out_ref, self.own, self.send, self.recv = out_ref, own, send, recv
+        self.zn, self.half, self.zlo, self.zhi = zn, rows // 2, zlo, zhi
+        self.z, self.x, self.y, self.c = coords()
+        z, x, y, c = self.z, self.x, self.y, self.c
+        self.to_x = place(z, 1 - x, y, c)
+        self.to_y = place(z, x, 1 - y, c)
+        self.to_c = place(z, x, y, 1 - c)
+        self.turns = 2 * zn + 1
+
+    def slot(self, zp, xp, yp, cp):
+        return (((zp - self.zlo) * 2 + xp) * 2 + yp) * 2 + cp
+
+    def whole(self, zp, xp, yp):
+        return self.out_ref.at[self.slot(zp, xp, yp, self.c)]
+
+    def upper(self, zp, xp, yp):
+        return self.out_ref.at[self.slot(zp, xp, yp, self.c), pl.ds(0, self.half)]
+
+    def lower(self, zp, xp, yp):
+        return self.out_ref.at[self.slot(zp, xp, yp, self.c), pl.ds(self.half, self.half)]
+
+    def cp(self, ref, zp, s, r, device):
+        i = zp - self.zlo
+        return remote(ref, ref, self.send.at[i, s], self.recv.at[i, r], device)
+
+    def right(self, zp):
+        return self.cp(self.whole(zp, self.x, self.y), zp, 0, 0, place(self.z + 1, self.x, self.y, self.c))
+
+    def left(self, zp):
+        return self.cp(self.whole(zp, self.x, self.y), zp, 1, 0, place(self.z - 1, self.x, self.y, self.c))
+
+    def first(self, zp):
+        ref = self.whole(zp, self.x, self.y)
+        return [
+            self.cp(ref, zp, 2, 1, self.to_x),
+            self.cp(ref, zp, 3, 2, self.to_y),
+            self.cp(ref, zp, 4, 3, self.to_c),
+        ]
+
+    def second_x(self, zp):
+        return [
+            self.cp(self.upper(zp, 1 - self.x, self.y), zp, 5, 4, self.to_y),
+            self.cp(self.whole(zp, 1 - self.x, self.y), zp, 6, 6, self.to_c),
+        ]
+
+    def second_y(self, zp):
+        return [
+            self.cp(self.lower(zp, self.x, 1 - self.y), zp, 7, 5, self.to_x),
+            self.cp(self.whole(zp, self.x, 1 - self.y), zp, 8, 7, self.to_c),
+        ]
+
+    def third_a(self, zp):
+        return self.cp(self.upper(zp, 1 - self.x, 1 - self.y), zp, 9, 8, self.to_c)
+
+    def third_b(self, zp):
+        return self.cp(self.lower(zp, 1 - self.x, 1 - self.y), zp, 10, 9, self.to_c)
+
+    def arrival(self, ref, zp, r):
+        self.cp(ref, zp, 0, r, self.to_c).wait_recv()
+
+    def keep(self, lsem):
+        @pl.when((self.z >= self.zlo) & (self.z < self.zhi))
+        def _():
+            copy = pltpu.make_async_copy(self.own, self.whole(self.z, self.x, self.y), lsem)
+            copy.start()
+            copy.wait()
+
+    def valid(self, tau):
+        zp = order_at(tau, self.z)
+        ok = (tau >= 0) & (tau < 2 * self.zn - 1) & (zp >= self.zlo) & (zp < self.zhi)
+        return zp, ok
+
+    def turn(self, tau):
+        z, x, y = self.z, self.x, self.y
+        zp, ok = self.valid(tau)
+
+        @pl.when(ok)
+        def _():
+            pl.when(tau > 0)(lambda: self.arrival(self.whole(zp, x, y), zp, 0))
+            pl.when((zp <= z) & (z < self.zn - 1))(lambda: self.right(zp).start())
+            pl.when((zp >= z) & (z > 0))(lambda: self.left(zp).start())
+            for item in self.first(zp):
+                item.start()
+
+        zq, ok_two = self.valid(tau - 1)
+
+        @pl.when(ok_two)
+        def _():
+            self.arrival(self.whole(zq, 1 - x, y), zq, 1)
+            for item in self.second_x(zq):
+                item.start()
+            self.arrival(self.whole(zq, x, 1 - y), zq, 2)
+            for item in self.second_y(zq):
+                item.start()
+
+        zr, ok_three = self.valid(tau - 2)
+
+        @pl.when(ok_three)
+        def _():
+            self.arrival(self.upper(zr, 1 - x, 1 - y), zr, 4)
+            self.third_a(zr).start()
+            self.arrival(self.lower(zr, 1 - x, 1 - y), zr, 5)
+            self.third_b(zr).start()
+
+    def pump(self, low, high):
+        def one(tau, carry):
+            self.turn(tau)
+            return carry
+
+        lax.fori_loop(low, high, one, 0)
+
+    def arrived(self):
+        x, y, far = self.x, self.y, 1 - self.c
+        half = self.half
+
+        def one(i, carry):
+            zp = self.zlo + i
+            ref = self.out_ref
+            self.arrival(ref.at[self.slot(zp, x, y, far)], zp, 3)
+            self.arrival(ref.at[self.slot(zp, 1 - x, y, far)], zp, 6)
+            self.arrival(ref.at[self.slot(zp, x, 1 - y, far)], zp, 7)
+            self.arrival(ref.at[self.slot(zp, 1 - x, 1 - y, far), pl.ds(0, half)], zp, 8)
+            self.arrival(ref.at[self.slot(zp, 1 - x, 1 - y, far), pl.ds(half, half)], zp, 9)
+            return carry
+
+        lax.fori_loop(0, self.zhi - self.zlo, one, 0)
+
+    def sent(self):
+        z = self.z
+
+        def one(i, carry):
+            zp = self.zlo + i
+            pl.when((zp <= z) & (z < self.zn - 1))(lambda: self.right(zp).wait_send())
+            pl.when((zp >= z) & (z > 0))(lambda: self.left(zp).wait_send())
+            for item in self.first(zp) + self.second_x(zp) + self.second_y(zp):
+                item.wait_send()
+            self.third_a(zp).wait_send()
+            self.third_b(zp).wait_send()
+            return carry
+
+        lax.fori_loop(0, self.zhi - self.zlo, one, 0)
+
+
+class KeyExchange:
+    def __init__(self, kv_ref, all_ref, send, recv, lsem, parts):
         z, x, y, c = coords()
-        bar = pltpu.get_barrier_semaphore()
-
-        def hello(device):
-            pl.semaphore_signal(bar, inc=1, device_id=device, device_id_type=MESH)
-
-        hello(place(z, 1 - x, y, c))
-        hello(place(z, x, 1 - y, c))
-        hello(place(z, x, y, 1 - c))
-        pl.when(z > 0)(lambda: hello(place(z - 1, x, y, c)))
-        pl.when(z < zn - 1)(lambda: hello(place(z + 1, x, y, c)))
-
-        shift = lax.rem(share * (((z * 2 + x) * 2 + y) * 2 + c), LANES)
-        lane = lax.broadcasted_iota(jnp.int32, (step, LANES), 1)
-
-        def align(i, carry):
-            now = pltpu.roll(x_ref[pl.ds(8 + i * step, step), :], shift, 1)
-            before = pltpu.roll(x_ref[pl.ds(7 + i * step, step), :], shift, 1)
-            own[pl.ds(i * step, step), :] = jnp.where(lane >= shift, now, before).astype(bf16)
-            return carry
-
-        lax.fori_loop(0, rows // step, align, 0)
-        pl.semaphore_wait(
-            bar, 3 + (z > 0).astype(jnp.int32) + (z < zn - 1).astype(jnp.int32)
-        )
-
-        def slot(zp, xp, yp, cp):
-            return (((zp - zlo) * 2 + xp) * 2 + yp) * 2 + cp
-
-        def whole(zp, xp, yp):
-            return out_ref.at[slot(zp, xp, yp, c)]
-
-        def upper(zp, xp, yp):
-            return out_ref.at[slot(zp, xp, yp, c), pl.ds(0, half)]
-
-        def lower(zp, xp, yp):
-            return out_ref.at[slot(zp, xp, yp, c), pl.ds(half, half)]
-
-        to_x = place(z, 1 - x, y, c)
+        rows = kv_ref.shape[0]
+        piece = rows // parts
         to_y = place(z, x, 1 - y, c)
         to_c = place(z, x, y, 1 - c)
-
-        def cp(ref, zp, s, r, device):
-            return remote(ref, ref, send.at[zp - zlo, s], recv.at[zp - zlo, r], device)
-
-        def right(zp):
-            return cp(whole(zp, x, y), zp, 0, 0, place(z + 1, x, y, c))
-
-        def left(zp):
-            return cp(whole(zp, x, y), zp, 1, 0, place(z - 1, x, y, c))
-
-        def first(zp):
-            ref = whole(zp, x, y)
-            return [cp(ref, zp, 2, 1, to_x), cp(ref, zp, 3, 2, to_y), cp(ref, zp, 4, 3, to_c)]
-
-        def second_x(zp):
-            return [
-                cp(upper(zp, 1 - x, y), zp, 5, 4, to_y),
-                cp(whole(zp, 1 - x, y), zp, 6, 6, to_c),
-            ]
-
-        def second_y(zp):
-            return [
-                cp(lower(zp, x, 1 - y), zp, 7, 5, to_x),
-                cp(whole(zp, x, 1 - y), zp, 8, 7, to_c),
-            ]
-
-        def third_a(zp):
-            return cp(upper(zp, 1 - x, 1 - y), zp, 9, 8, to_c)
-
-        def third_b(zp):
-            return cp(lower(zp, 1 - x, 1 - y), zp, 10, 9, to_c)
-
-        def arrival(ref, zp, r):
-            cp(ref, zp, 0, r, to_c).wait_recv()
-
-        mine = (z >= zlo) & (z < zhi)
-
-        @pl.when(mine)
-        def _():
-            keep = pltpu.make_async_copy(own, whole(z, x, y), lsem)
-            keep.start()
-            keep.wait()
-
-        def valid(zp):
-            return (zp >= zlo) & (zp < zhi)
-
-        def stage_one(tau):
-            zp = order_at(tau, z)
-
-            @pl.when(valid(zp))
-            def _():
-                pl.when(tau > 0)(lambda: arrival(whole(zp, x, y), zp, 0))
-                pl.when((zp <= z) & (z < zn - 1))(lambda: right(zp).start())
-                pl.when((zp >= z) & (z > 0))(lambda: left(zp).start())
-                for item in first(zp):
-                    item.start()
-
-        def stage_two(tau):
-            zp = order_at(tau, z)
-
-            @pl.when((tau >= 0) & valid(zp))
-            def _():
-                arrival(whole(zp, 1 - x, y), zp, 1)
-                for item in second_x(zp):
-                    item.start()
-                arrival(whole(zp, x, 1 - y), zp, 2)
-                for item in second_y(zp):
-                    item.start()
-
-        def stage_three(tau):
-            zp = order_at(tau, z)
-
-            @pl.when((tau >= 0) & valid(zp))
-            def _():
-                arrival(upper(zp, 1 - x, 1 - y), zp, 4)
-                third_a(zp).start()
-                arrival(lower(zp, 1 - x, 1 - y), zp, 5)
-                third_b(zp).start()
-
-        total = 2 * zn - 1
-
-        def turn(tau, carry):
-            pl.when(tau < total)(lambda: stage_one(tau))
-            pl.when(tau - 1 < total)(lambda: stage_two(tau - 1))
-            stage_three(tau - 2)
-            return carry
-
-        lax.fori_loop(0, total + 2, turn, 0)
-
-        def finish(i, carry):
-            zp = zlo + i
-            pl.when((zp <= z) & (z < zn - 1))(lambda: right(zp).wait_send())
-            pl.when((zp >= z) & (z > 0))(lambda: left(zp).wait_send())
-            for item in first(zp) + second_x(zp) + second_y(zp) + [third_a(zp), third_b(zp)]:
-                item.wait_send()
-            far = 1 - c
-            arrival(out_ref.at[slot(zp, x, y, far)], zp, 3)
-            arrival(out_ref.at[slot(zp, 1 - x, y, far)], zp, 6)
-            arrival(out_ref.at[slot(zp, x, 1 - y, far)], zp, 7)
-            arrival(out_ref.at[slot(zp, 1 - x, 1 - y, far), pl.ds(0, half)], zp, 8)
-            arrival(out_ref.at[slot(zp, 1 - x, 1 - y, far), pl.ds(half, half)], zp, 9)
-            return carry
-
-        lax.fori_loop(0, nz, finish, 0)
-
-    return pl.pallas_call(
-        body,
-        out_shape=jax.ShapeDtypeStruct((nz * 8, rows, LANES), bf16),
-        in_specs=[vmem_spec()],
-        out_specs=any_spec(),
-        scratch_shapes=[
-            pltpu.VMEM((rows, LANES), bf16),
-            pltpu.SemaphoreType.DMA((nz, 11)),
-            pltpu.SemaphoreType.DMA((nz, 10)),
-            pltpu.SemaphoreType.DMA,
-        ],
-        compiler_params=pltpu.CompilerParams(
-            collective_id=1, has_side_effects=True, vmem_limit_bytes=40 * MIB
-        ),
-    )(master_pad)
-
-
-def unpack_weights(slots, layer, rows, share):
-    per_layer = slots.shape[0] // 2
+        mine = y * 2 + c
+        beyond = (1 - y) * 2 + c
+        self.parts = parts
+
+        def part(row, k):
+            return all_ref.at[pl.ds(pl.multiple_of(row * rows, rows) + k * piece, piece)]
+
+        self.keep = pltpu.make_async_copy(
+            kv_ref, all_ref.at[pl.ds(pl.multiple_of(mine * rows, rows), rows)], lsem
+        )
+        self.own_y, self.own_c, self.pass_c = [], [], []
+        for k in range(parts):
+            src, dst = kv_ref.at[pl.ds(k * piece, piece)], part(mine, k)
+            self.own_y.append(remote(src, dst, send.at[0, k], recv.at[0, k], to_y))
+            self.own_c.append(remote(src, dst, send.at[1, k], recv.at[1, k], to_c))
+            ref = part(beyond, k)
+            self.pass_c.append(remote(ref, ref, send.at[2, k], recv.at[2, k], to_c))
+
+    def start(self):
+        self.keep.start()
+        for item in self.own_y + self.own_c:
+            item.start()
+
+    def forward(self):
+        for k in range(self.parts):
+            self.own_y[k].wait_recv()
+            self.pass_c[k].start()
+
+    def finish(self):
+        for k in range(self.parts):
+            self.own_c[k].wait_recv()
+            self.pass_c[k].wait_recv()
+        for item in self.own_y + self.own_c + self.pass_c:
+            item.wait_send()
+        self.keep.wait()
+
+
+def fill_flat(slots, flat, rows, share, low, high):
     step = chunk_rows(rows)
-    depth = LAYER_ROWS + rows
-
-    def body(s_ref, qkv_ref, out_ref, gu_ref, down_ref, gains_ref, flat, gate_up):
-        i = pl.program_id(0)
+
+    def one(i, carry):
         start = lax.div(share * i, LANES)
         shift = lax.rem(share * i, LANES)
         edge = flat[pl.ds(start, 1), :]
 
-        def fill(j, carry):
-            flat[pl.ds(start + j * step, step), :] = s_ref[0, pl.ds(j * step, step), :].astype(f32)
-            return carry
+        def fill(j, inner):
+            flat[pl.ds(start + j * step, step), :] = slots[i, pl.ds(j * step, step), :].astype(f32)
+            return inner
 
         lax.fori_loop(0, rows // step, fill, 0)
 
@@ -285,59 +302,52 @@
         def _():
             flat[pl.ds(start, 1), :] = flat[pl.ds(start, 1), :] + edge
 
-        @pl.when(i == per_layer - 1)
-        def _():
-            for col in range(12):
-                qkv_ref[:, 128 * col : 128 * col + 128] = flat[
-                    pl.ds(col, D, stride=12), :
-                ].astype(bf16)
-            for col in range(4):
-                out_ref[:, 128 * col : 128 * col + 128] = flat[
-                    pl.ds(BASE_OUT + col, D, stride=4), :
-                ].astype(bf16)
-                down_ref[0:FF, 128 * col : 128 * col + 128] = flat[
-                    pl.ds(BASE_DOWN + col, FF, stride=4), :
-                ].astype(bf16)
-                gains_ref[:, 128 * col : 128 * col + 128] = flat[
-                    pl.ds(BASE_GAINS + col, 2, stride=4), :
-                ]
-            down_ref[FF:FFP, :] = jnp.zeros((FFP - FF, D), bf16)
-            lane = lax.broadcasted_iota(jnp.int32, (64, LANES), 1)
-            for r in range(8):
-                for part in range(2):
-                    for tile in range(TILES):
-                        first = GU_ROW * r + FF * part + LANES * tile
-                        q, s = first // LANES, first % LANES
-                        value = flat[pl.ds(BASE_GU + q, 64, stride=PERIOD), :]
-                        if s:
-                            after = flat[pl.ds(BASE_GU + q + 1, 64, stride=PERIOD), :]
-                            value = jnp.where(
-                                lane < LANES - s,
-                                pltpu.roll(value, LANES - s, 1),
-                                pltpu.roll(after, LANES - s, 1),
-                            )
-                        if tile == TILES - 1:
-                            value = jnp.where(lane < FF - LANES * tile, value, 0.0)
-                        gate_up[2 * tile + part, pl.ds(r, 64, stride=8), :] = value
-            for k in range(2 * TILES):
-                gu_ref[:, 128 * k : 128 * k + 128] = gate_up[k].astype(bf16)
-
-    shapes = [
-        ((D, 3 * D), bf16),
-        ((D, D), bf16),
-        ((D, 2 * FFP), bf16),
-        ((FFP, D), bf16),
-        ((2, D), f32),
-    ]
-    return pl.pallas_call(
-        body,
-        grid=(per_layer,),
-        out_shape=[jax.ShapeDtypeStruct(s, d) for s, d in shapes],
-        in_specs=[pl.BlockSpec((1, rows, LANES), lambda i: (layer * per_layer + i, 0, 0))],
-        out_specs=[pl.BlockSpec(s, lambda i: (0, 0)) for s, _ in shapes],
-        scratch_shapes=[pltpu.VMEM((depth, LANES), f32), pltpu.VMEM((2 * TILES, D, LANES), f32)],
-        compiler_params=pltpu.CompilerParams(vmem_limit_bytes=60 * MIB),
-    )(slots)
+        return carry
+
+    lax.fori_loop(low, high, one, 0)
+
+
+def take_qkv(flat, qkv_ref, low, high):
+    for col in range(low, high):
+        qkv_ref[:, 128 * col : 128 * col + 128] = flat[pl.ds(col, D, stride=12), :].astype(bf16)
+
+
+def take_out(flat, out_ref, gains_ref):
+    for col in range(4):
+        span = slice(128 * col, 128 * col + 128)
+        out_ref[:, span] = flat[pl.ds(BASE_OUT + col, D, stride=4), :].astype(bf16)
+        gains_ref[:, span] = flat[pl.ds(BASE_GAINS + col, 2, stride=4), :]
+
+
+def take_down(flat, down_ref):
+    for col in range(4):
+        span = slice(128 * col, 128 * col + 128)
+        down_ref[0:FF, span] = flat[pl.ds(BASE_DOWN + col, FF, stride=4), :].astype(bf16)
+    down_ref[FF:FFP, :] = jnp.zeros((FFP - FF, D), bf16)
+
+
+def take_gate_up(flat, gate_up, r):
+    lane = lax.broadcasted_iota(jnp.int32, (64, LANES), 1)
+    for part in range(2):
+        for tile in range(TILES):
+            first = GU_ROW * r + FF * part + LANES * tile
+            q, s = first // LANES, first % LANES
+            value = flat[pl.ds(BASE_GU + q, 64, stride=PERIOD), :]
+            if s:
+                after = flat[pl.ds(BASE_GU + q + 1, 64, stride=PERIOD), :]
+                value = jnp.where(
+                    lane < LANES - s,
+                    pltpu.roll(value, LANES - s, 1),
+                    pltpu.roll(after, LANES - s, 1),
+                )
+            if tile == TILES - 1:
+                value = jnp.where(lane < FF - LANES * tile, value, 0.0)
+            gate_up[2 * tile + part, pl.ds(r, 64, stride=8), :] = value
+
+
+def place_gate_up(gate_up, gu_ref):
+    for k in range(2 * TILES):
+        gu_ref[:, 128 * k : 128 * k + 128] = gate_up[k].astype(bf16)
 
 
 def gate_up_segments(q):
@@ -668,13 +678,119 @@
     return mm_nt(eboth_ref[...], gu_ref[...])
 
 
-def stage_heads(hidden, w_qkv, cos, sin):
-    rows = hidden.shape[0]
-
-    def body(a_ref, w_ref, c_ref, s_ref, q_ref, kv_ref):
-        project_heads(a_ref[...], w_ref, c_ref, s_ref, q_ref, kv_ref)
-
-    return local_call(body, [((rows, D), bf16), ((rows, 2 * D), bf16)], [hidden, w_qkv, cos, sin])
+def stage_head(master_pad, hidden, cos, sin, zn, rows, share):
+    tokens = hidden.shape[0]
+    step = chunk_rows(rows)
+    per_layer = zn * 4
+    half_zn = zn // 2
+    depth = LAYER_ROWS + rows
+    parts = 4
+
+    def body(
+        x_ref, h_ref, c_ref, s_ref,
+        wq0, wo0, wg0, wd0, g0, wq1, wo1, wg1, wd1, g1, q_ref, all_ref,
+        own, slots0, slots1, flat, gate_up, kv, send0, recv0, send1, recv1, ksend, krecv, lsem,
+    ):
+        z, x, y, c = coords()
+        bar = pltpu.get_barrier_semaphore()
+
+        def hello(device):
+            pl.semaphore_signal(bar, inc=1, device_id=device, device_id_type=MESH)
+
+        hello(place(z, 1 - x, y, c))
+        hello(place(z, x, 1 - y, c))
+        hello(place(z, x, y, 1 - c))
+        pl.when(z > 0)(lambda: hello(place(z - 1, x, y, c)))
+        pl.when(z < zn - 1)(lambda: hello(place(z + 1, x, y, c)))
+
+        shift = lax.rem(share * (((z * 2 + x) * 2 + y) * 2 + c), LANES)
+        lane = lax.broadcasted_iota(jnp.int32, (step, LANES), 1)
+
+        def align(i, carry):
+            now = pltpu.roll(x_ref[pl.ds(8 + i * step, step), :], shift, 1)
+            before = pltpu.roll(x_ref[pl.ds(7 + i * step, step), :], shift, 1)
+            own[pl.ds(i * step, step), :] = jnp.where(lane >= shift, now, before).astype(bf16)
+            return carry
+
+        lax.fori_loop(0, rows // step, align, 0)
+        pl.semaphore_wait(
+            bar, 3 + (z > 0).astype(jnp.int32) + (z < zn - 1).astype(jnp.int32)
+        )
+        zero = Gather(slots0, own, send0, recv0, zn, rows, 0, half_zn)
+        one = Gather(slots1, own, send1, recv1, zn, rows, half_zn, zn)
+        exchange = KeyExchange(kv, all_ref, ksend, krecv, lsem.at[1], parts)
+        zero.keep(lsem.at[0])
+        one.keep(lsem.at[0])
+        zero.turn(0)
+        one.turn(0)
+        zero.pump(1, zero.turns)
+        zero.arrived()
+
+        sites = 9
+        calls = []
+
+        def pump():
+            k = len(calls)
+            calls.append(k)
+            total = one.turns - 1
+            one.pump(1 + total * k // sites, 1 + total * (k + 1) // sites)
+
+        fill_flat(slots0, flat, rows, share, 0, per_layer)
+        pump()
+        take_qkv(flat, wq0, 0, 12)
+        pump()
+        project_heads(h_ref[...], wq0, c_ref, s_ref, q_ref, kv)
+        exchange.start()
+        pump()
+        take_out(flat, wo0, g0)
+        take_down(flat, wd0)
+        pump()
+        for r in range(8):
+            take_gate_up(flat, gate_up, r)
+            if r % 2 == 1:
+                pump()
+        place_gate_up(gate_up, wg0)
+        exchange.forward()
+        pump()
+        one.arrived()
+        fill_flat(slots1, flat, rows, share, 0, per_layer)
+        take_qkv(flat, wq1, 0, 12)
+        take_out(flat, wo1, g1)
+        take_down(flat, wd1)
+        for r in range(8):
+            take_gate_up(flat, gate_up, r)
+        place_gate_up(gate_up, wg1)
+        exchange.finish()
+        zero.sent()
+        one.sent()
+
+    layer = [((D, 3 * D), bf16), ((D, D), bf16), ((D, 2 * FFP), bf16), ((FFP, D), bf16), ((2, D), f32)]
+    outs = layer + layer + [((tokens, D), bf16), ((4 * tokens, 2 * D), bf16)]
+    ins = [master_pad, hidden, cos, sin]
+    return pl.pallas_call(
+        body,
+        out_shape=[jax.ShapeDtypeStruct(s, d) for s, d in outs],
+        in_specs=[vmem_spec()] * len(ins),
+        out_specs=[vmem_spec()] * len(outs),
+        scratch_shapes=[
+            pltpu.VMEM((rows, LANES), bf16),
+            pltpu.VMEM((per_layer, rows, LANES), bf16),
+            pltpu.VMEM((per_layer, rows, LANES), bf16),
+            pltpu.VMEM((depth, LANES), f32),
+            pltpu.VMEM((2 * TILES, D, LANES), f32),
+            pltpu.VMEM((tokens, 2 * D), bf16),
+            pltpu.SemaphoreType.DMA((half_zn, 11)),
+            pltpu.SemaphoreType.DMA((half_zn, 10)),
+            pltpu.SemaphoreType.DMA((half_zn, 11)),
+            pltpu.SemaphoreType.DMA((half_zn, 10)),
+            pltpu.SemaphoreType.DMA((3, parts)),
+            pltpu.SemaphoreType.DMA((3, parts)),
+            pltpu.SemaphoreType.DMA((2,)),
+        ],
+        compiler_params=pltpu.CompilerParams(
+            collective_id=1, has_side_effects=True, vmem_limit_bytes=60 * MIB
+        ),
+    )(*ins)
 
 
 def stage_first(length, hidden, q, kv, w_out, w_gu, w_down, gains, next_gains, w_qkv, cos, sin):
@@ -1162,9 +1278,6 @@
         return jnp.pad(flat, (lead * LANES, rows * LANES - share)).reshape(rows + lead, LANES)
 
     master_pad = pad(master, 8)
-    slots = gather_weights(master_pad, zn, rows, share, 0, zn)
-    wq0, wo0, wg0, wd0, g0 = unpack_weights(slots, 0, rows, share)
-    wq1, wo1, wg1, wd1, g1 = unpack_weights(slots, 1, rows, share)
     cos, sin = rope_rows(tokens)
     hidden = hidden_in.reshape(tokens, width)
 
@@ -1174,8 +1287,9 @@
     def collect(dkv):
         return collect_keys(dkv.reshape(4, tokens, 2 * width))
 
-    q0, kv0 = stage_heads(hidden, wq0, cos, sin)
-    kv0 = join(kv0)
+    wq0, wo0, wg0, wd0, g0, wq1, wo1, wg1, wd1, g1, q0, kv0 = stage_head(
+        master_pad, hidden, cos, sin, zn, rows, share
+    )
     p0, ctx0, r1, b0, both0, units0, r2, second, a1, q1, kv1 = stage_first(
         lengths, hidden, q0, kv0, wo0, wg0, wd0, g0, g1, wq1, cos, sin
     )

time: 354 us -> 348 us (0.983)
  local copies, waits for them, and re-layouts: 20.7 us -> 14.6 us
    pallas_call x2 -> x1, Pallas kernels: 31.1 us -> 16 us  [exchange_keys(): pl.pallas_call(body, out_shape=jax.ShapeDtypeStruct((4, rows, width), kv....]
    unnamed x34 -> x26, local copies, waits for them, and re-layouts: 12.6 us -> 5.58 us
    pallas_call x3 -> x2, Pallas kernels: 23.5 us -> 29.9 us  [local_call(): pl.pallas_call(body, out_shape=[jax.ShapeDtypeStruct(s, d) for s, d in ou...]
    pallas_call x1, Pallas kernels: 80 us -> 83.7 us  [reduce_and_update(): pl.pallas_call(body, out_shape=[flat, flat, flat, jax.ShapeDtypeStruct((8...]
    pallas_call x3 -> x1, Pallas kernels: 96.8 us -> 99 us  [stage_head(): pl.pallas_call(body, out_shape=[jax.ShapeDtypeStruct(s, d) for s, d in ou...]
where the time goes in v2:
time: 348 us; the launch traced here: 344 us
  Pallas kernels  323 us (93%)
  local copies, waits for them, and re-layouts  14.6 us (4%)
  other arithmetic  5.17 us (1%)
    pallas_call x1, Pallas kernels, stage_head(): pl.pallas_call(body, out_shape=[jax.ShapeDtypeStruct(s, d) for s, d in ou...  99 us
    pallas_call x1, Pallas kernels, reduce_and_update(): pl.pallas_call(body, out_shape=[flat, flat, flat, jax.ShapeDtypeStruct((8...  83.7 us
    pallas_call x2, Pallas kernels, collect_keys(): pl.pallas_call(body, out_shape=jax.ShapeDtypeStruct((rows, width), bf16),...  31.1 us
    pallas_call x2, Pallas kernels, local_call(): pl.pallas_call(body, out_shape=[jax.ShapeDtypeStruct(s, d) for s, d in ou...  29.9 us
    pallas_call x2, Pallas kernels, weight_grads(): pl.pallas_call(body, grid=(per_layer,), out_shape=jax.ShapeDtypeStruct((p...  27.7 us
    pallas_call x1, Pallas kernels, stage_second(): pl.pallas_call(body, out_shape=[jax.ShapeDtypeStruct(s, d) for s, d in ou...  20.4 us
    pallas_call x1, Pallas kernels, exchange_keys(): pl.pallas_call(body, out_shape=jax.ShapeDtypeStruct((4, rows, width), kv....  16 us
    pallas_call x1, Pallas kernels, stage_first(): pl.pallas_call(body, out_shape=[jax.ShapeDtypeStruct(s, d) for s, d in ou...  15.1 us

profile of v2, /device:TPU:0, one launch (start us, length us, event | category | flops | bytes accessed | tf_op | source)
XLA Modules:
  0.0 344.3 jit_solution(2826226604642025368)
XLA Ops:
  1.2 1.0 pad_maximum_fusion
  2.2 2.1 pad_bitcast_fusion.x_ref.m_ref
  4.3 99.0 %shard_map.125 = (bf16[512,1536]{1,0:T(8,128)(2,1)}, bf16[512,512]{1,0:T(8,128)(2,1)}, bf16[512,2816]{1,0:T(8,128)(2,1)}, bf16[1408,512]{1,0:T(8,128)(2,1)}, f32...) custom-call(f32[1576,128]{1,0:T(8,128)} %pad_bitcast_fusion.x_ref.m_, ...), custom_call_target="tpu_custom_call" | custom-call | tf_op jit(solution)/shard_map/pallas_call | solution.py:770
  104.0 15.1 %shard_map.126 = (bf16[8,256,1024]{2,1,0:T(8,128)(2,1)}, bf16[256,512]{1,0:T(8,128)(2,1)}, f32[256,512]{1,0:T(8,128)}, bf16[256,512]{1,0:T(8,128)(2,1)}, f32[256...) custom-call(s32[1]{0:T(128)S(6)} %copy.15.l_ref, ...), custom_call_target="tpu_custom_call" | custom-call | tf_op jit(solution)/shard_map/pallas_call | solution.py:832
  119.1 1.0 copy-done.5
  120.2 16.0 %shard_map.127 = bf16[4,256,1024]{2,1,0:T(8,128)(2,1)S(1)} custom-call(bf16[256,1024]{1,0:T(8,128)(2,1)S(1)} %copy-done.5), custom_call_target="tpu_custom_call" | custom-call | tf_op jit(solution)/shard_map/pallas_call | solution.py:471
  136.2 1.3 copy-done
  137.5 20.4 %shard_map.128 = (f32[256,512]{1,0:T(8,128)}, bf16[256,512]{1,0:T(8,128)(2,1)}, bf16[256,512]{1,0:T(8,128)(2,1)}, bf16[256,1408]{1,0:T(8,128)(2,1)}, bf16[256,28...) custom-call(s32[1]{0:T(128)S(6)} %copy.15.l_ref, ...), custom_call_target="tpu_custom_call" | custom-call | tf_op jit(solution)/shard_map/pallas_call | solution.py:884
  157.8 1.6 copy-done.3
  159.4 15.8 %shard_map.129.ekv_ref = bf16[256,1024]{1,0:T(8,128)(2,1)S(1)} custom-call(bf16[4,256,1024]{2,1,0:T(8,128)(2,1)S(1)} %bitcast.19), custom_call_target="tpu_custom_call" | custom-call | tf_op jit(solution)/shard_map/pallas_call | solution.py:539
  175.2 0.8 copy-done.1
  176.1 26.5 %shard_map.130 = (bf16[256,1536]{1,0:T(8,128)(2,1)}, bf16[256,2816]{1,0:T(8,128)(2,1)}, bf16[256,512]{1,0:T(8,128)(2,1)}, bf16[256,512]{1,0:T(8,128)(2,1)}, f32[...) custom-call(bf16[256,512]{1,0:T(8,128)(2,1)} %get-tuple-element.72.eq_ref, ...), custom_call_target="tpu_custom_call" | custom-call | tf_op jit(solution)/shard_map/pallas_call | solution.py:62
  202.6 0.7 pad_maximum_fusion.2
  205.2 13.9 %shard_map.134.g1_ref = bf16[16,1568,128]{2,1,0:T(8,128)(2,1)} custom-call(bf16[256,512]{1,0:T(8,128)(2,1)} %get-tuple-element.92.a_ref, bf16[256,1536]{1,0:T(8,128)(2,1)} %get-tuple-element.93.lin_ref, bf16[256,512]{1,0:T(8,128)(2,1)} %get-tuple-element.94.ctx_ref, bf16[256,512]{1,0:T(8,128)(2,1)} %get-tuple-element.95.ea_ref, ...), custom_call_target="tpu_custom_call" | custom-call | tf_op jit(solution)/shard_map/pallas_call | solution.py:418
  219.1 15.3 %shard_map.131.ekv_ref = bf16[256,1024]{1,0:T(8,128)(2,1)S(1)} custom-call(bf16[4,256,1024]{2,1,0:T(8,128)(2,1)S(1)} %bitcast.18), custom_call_target="tpu_custom_call" | custom-call | tf_op jit(solution)/shard_map/pallas_call | solution.py:539
  234.4 0.8 copy-done.4
  235.2 3.4 shard_map.132
  239.1 13.9 %shard_map.133.g0_ref = bf16[16,1568,128]{2,1,0:T(8,128)(2,1)} custom-call(bf16[256,512]{1,0:T(8,128)(2,1)} %bitcast.22, bf16[256,1536]{1,0:T(8,128)(2,1)} %get-tuple-element.84.lin_ref, bf16[256,512]{1,0:T(8,128)(2,1)} %get-tuple-element.85.ctx_ref, bf16[256,512]{1,0:T(8,128)(2,1)} %get-tuple-element.86.ea_ref, bf16[256,512]{1,0:T(8,128)(2,1)} %get-tuple-element.87.b_ref, ...), custom_call_target="tpu_custom_call" | custom-call | tf_op jit(solution)/shard_map/pallas_call | solution.py:418
  253.0 1.4 pad_bitcast_fusion.1
  254.4 83.7 %shard_map.135 = (f32[1568,128]{1,0:T(8,128)}, f32[1568,128]{1,0:T(8,128)}, f32[1568,128]{1,0:T(8,128)}, f32[8,128]{1,0:T(8,128)}, f32[16,128]{1,0:T(8,128)}) custom-call(bf16[16,1568,128]{2,1,0:T(8,128)(2,1)} %shard_map.133.g0_ref, bf16[16,1568,128]{2,1,0:T(8,128)(2,1)} %shard_map.134.g1_ref, f32[16,128]{1,0:T(8,128)} %reshape.80.gp_ref, ...), custom_call_target="tpu_custom_call" | custom-call | tf_op jit(solution)/shard_map/pallas_call | solution.py:1222
  338.1 2.3 fusion.1
  340.4 0.9 slice.26
  341.3 0.9 slice.27
  342.9 1.2 slice.24
  (29 shorter events, 3.7 us)
Async XLA Ops:
  119.1 1.0 copy-start.5
  136.2 1.3 copy-start
  157.8 1.6 copy-start.3
  175.2 0.9 copy-start.1
  176.1 26.5 %copy-start.12 = (f32[1,512]{1,0:T(1,128)S(1)}, f32[1,512]{1,0:T(1,128)}, u32[]{:S(2)}) copy-start(f32[1,512]{1,0:T(1,128)} %get-tuple-element.100) | copy-start | bytes 6148
  205.2 13.9 %copy-start.2 = (bf16[1024,1024]{1,0:T(8,128)(2,1)S(1)}, bf16[1024,1024]{1,0:T(8,128)(2,1)}, u32[]{:S(2)}) copy-start(bf16[1024,1024]{1,0:T(8,128)(2,1)} %get-tuple-element.80) | copy-start | bytes 6291460
  234.4 0.8 copy-start.4
  235.2 3.4 copy-start.10
  239.1 13.9 %copy-start.6 = (f32[196928]{0:T(1024)S(1)}, f32[196928]{0:T(1024)}, u32[]{:S(2)}) copy-start(f32[196928]{0:T(1024)} %param.11) | copy-start | bytes 2363140
  239.1 13.9 %copy-start.7 = (f32[196928]{0:T(1024)S(1)}, f32[196928]{0:T(1024)}, u32[]{:S(2)}) copy-start(f32[196928]{0:T(1024)} %param.10) | copy-start | bytes 2363140
  338.0 2.4 copy-start.9
  338.0 3.3 copy-start.8
  338.1 4.2 %copy-start.11 = (f32[16,128]{1,0:T(8,128)S(1)}, f32[16,128]{1,0:T(8,128)}, u32[]{:S(2)}) copy-start(f32[16,128]{1,0:T(8,128)} %get-tuple-element.105) | copy-start | bytes 24580
